TPU v7x, 768 devices: a whole 4x8x12 slice. The times are simulated.
768 devices in a mesh: gx: 8 (over x, core), gy: 96 (over y, z).
Axes of the slice: x: 4, y: 8, z: 12, core: 2. Of those that a mesh axis runs over, the one named last changes fastest.
Arguments:
- density: float32 [8, 1536, 1024], P(None, 'gy', 'gx'), may hold values from 0.5 to 2
- momentum: float32 [3, 8, 1536, 1024], P(None, None, 'gy', 'gx'), may hold values from -1.8 to 1.8
- energy: float32 [8, 1536, 1024], P(None, 'gy', 'gx'), may hold values from 2.5 to 4
- solid_flags: int32 [8, 1536, 1024], P(None, 'gy', 'gx'), may hold values from 0 to 1, as said below
Outputs:
- advanced_state: float32 [5, 8, 1536, 1024], P(None, None, 'gy', 'gx')
Inputs may be any that keep to these rules, and one draw needn't show every extreme that they name: `solid_flags`: 1 marks a cell inside the vocal folds, 0 a fluid cell. In each plane of fixed z the folds occupy 1024 // 4 consecutive x positions, at the cells whose distance in y from a centre is at least an opening of 0 to 383 cells.
All inputs are finite; a program needn't handle non-finite values.
Results may differ from a plain program's by a relative error of at most 0.0003.
Values sent between devices are 32-bit elements; how exact they have to be, the bound alone decides.
No kernel may reach another device: no remote copies, remote signals or barrier semaphores. Data moves between devices by JAX's collectives and lax.ppermute only.
A program may use at most 32 MiB of HBM per device.

v0:
```python
import math

import jax
import jax.numpy as jnp
from jax import lax
from jax.sharding import PartitionSpec as P

gas_gamma = 1.4
step_size = 0.1
filter_alpha = 0.4999
third_part = 1.0 / 3.0


def extended(shard, sides, width):
    for axis, dim in sides:
        count, length = (lax.axis_size(axis), shard.shape[dim])
        up = [(i, (i + 1) % count) for i in range(count - 1)]
        down = [(j, i) for i, j in up]
        last = lax.slice_in_dim(shard, length - width, length, axis=dim)
        leading = lax.slice_in_dim(shard, 0, width, axis=dim)
        before = lax.ppermute(last, axis, up)
        after = lax.ppermute(leading, axis, down)
        shard = jnp.concatenate([before, shard, after], axis=dim)
    return shard


def prefix(shard, axis, combine, identity, reverse):
    count, position = (lax.axis_size(axis), lax.axis_index(axis))
    everything = jax.tree.map(lambda part: lax.all_gather(part, axis), shard)
    start = jax.tree.map(
        lambda part, zero: jnp.broadcast_to(jnp.asarray(zero, part.dtype), part.shape),
        shard,
        identity,
    )

    def step(k, before):
        at = count - 1 - k if reverse else k
        reached = at > position if reverse else at < position
        new = combine(before, jax.tree.map(lambda part: part[at], everything))
        return jax.tree.map(lambda a, b: jnp.where(reached, a, b), new, before)

    return lax.fori_loop(0, count, step, start)


def fluxes(density, momentum, energy):
    velocity = momentum[0] / density
    kinetic = (
        0.5
        * (momentum[0] * momentum[0] + momentum[1] * momentum[1] + momentum[2] * momentum[2])
        / density
    )
    pressure = (gas_gamma - 1.0) * (energy - kinetic)
    return jnp.stack(
        [
            momentum[0],
            momentum[0] * velocity + pressure,
            momentum[1] * velocity,
            momentum[2] * velocity,
            (energy + pressure) * velocity,
        ]
    )


def filter_weights():
    return [
        (193.0 + 126.0 * filter_alpha) / 256.0,
        (105.0 + 302.0 * filter_alpha) / 256.0,
        15.0 * (2.0 * filter_alpha - 1.0) / 64.0,
        45.0 * (1.0 - 2.0 * filter_alpha) / 512.0,
        5.0 * (2.0 * filter_alpha - 1.0) / 256.0,
        (1.0 - 2.0 * filter_alpha) / 512.0,
    ]


def eliminated(step_count):
    root_term = math.sqrt(1.0 - 4.0 * filter_alpha * filter_alpha)
    decay_ratio = (1.0 - root_term) / (1.0 + root_term)
    leading = 2.0 * filter_alpha / (1.0 + root_term)
    powered = jnp.exp(jnp.maximum(step_count, 0).astype(jnp.float32) * math.log(decay_ratio))
    return leading * (1.0 - powered) / (1.0 - powered * decay_ratio)


def compose(earlier, later):
    return (earlier[0] * later[0], later[0] * earlier[1] + later[1])


def local_pass(row_values, multiplier, divisor, offsets):
    carried = jnp.zeros_like(row_values[0])
    product = jnp.ones((), jnp.float32)
    partial_values = {}
    products = {}
    for offset in offsets:
        carried = multiplier[offset] * carried + row_values[offset] / divisor[offset]
        product = product * multiplier[offset]
        partial_values[offset] = carried
        products[offset] = product
    return (partial_values, products, carried, product)


def body(density, momentum, energy, solid_flags):
    planes, transverse, streamwise = density.shape
    streamwise_parts = lax.axis_size("gx")
    transverse_parts = lax.axis_size("gy")
    fluid_cells = (1 - solid_flags).astype(jnp.float32)
    flux_fields = fluxes(density, momentum, energy)
    flux_lines = flux_fields.reshape(-1, streamwise)
    streamwise_total = streamwise * streamwise_parts
    local_place = jnp.arange(streamwise)
    position = lax.axis_index("gx") * streamwise + local_place
    padded = jnp.pad(flux_lines, ((0, 0), (2, 2)))
    right_side = 7.0 / 9.0 * (
        padded[:, 3 : streamwise + 3] - padded[:, 1 : streamwise + 1]
    ) + 1.0 / 36.0 * (padded[:, 4 : streamwise + 4] - padded[:, 0:streamwise])
    closure_start = 0.5 * (
        -5.0 * flux_lines[:, 0:1] + 4.0 * flux_lines[:, 1:2] + flux_lines[:, 2:3]
    )
    closure_next = 0.75 * (flux_lines[:, 2:3] - flux_lines[:, 0:1])
    closure_penult = 0.75 * (
        flux_lines[:, streamwise - 1 : streamwise] - flux_lines[:, streamwise - 3 : streamwise - 2]
    )
    closure_end = 0.5 * (
        5.0 * flux_lines[:, streamwise - 1 : streamwise]
        - 4.0 * flux_lines[:, streamwise - 2 : streamwise - 1]
        - flux_lines[:, streamwise - 3 : streamwise - 2]
    )
    right_side = jnp.where(position == 0, closure_start, right_side)
    right_side = jnp.where(position == 1, closure_next, right_side)
    right_side = jnp.where(position == streamwise_total - 2, closure_penult, right_side)
    right_side = jnp.where(position == streamwise_total - 1, closure_end, right_side)
    near_ends = (position == 1) | (position == streamwise_total - 2)
    lower_band = jnp.where(
        position == streamwise_total - 1, 2.0, jnp.where(near_ends, 0.25, third_part)
    )
    lower_band = jnp.where(local_place == 0, 0.0, lower_band).astype(jnp.float32)
    upper_band = jnp.where(position == 0, 2.0, jnp.where(near_ends, 0.25, third_part))
    upper_band = jnp.where(local_place == streamwise - 1, 0.0, upper_band).astype(jnp.float32)
    diagonal = jnp.ones((streamwise,), jnp.float32)
    identity = jnp.eye(streamwise, dtype=jnp.float32)
    inverse = lax.linalg.tridiagonal_solve(lower_band, diagonal, upper_band, identity)
    plain_lower = jnp.where(local_place == 0, 0.0, third_part).astype(jnp.float32)
    plain_upper = jnp.where(local_place == streamwise - 1, 0.0, third_part).astype(jnp.float32)
    plain_column = lax.linalg.tridiagonal_solve(
        plain_lower, diagonal, plain_upper, identity[:, 0:1]
    )
    corner = plain_column[0, 0]
    scale_term = 1.0 / (1.0 - third_part * third_part * corner * corner)
    local_solution = lax.dot_general(
        right_side,
        inverse,
        (((1,), (1,)), ((), ())),
        precision=lax.Precision.HIGHEST,
        preferred_element_type=jnp.float32,
    )
    first_device = lax.axis_index("gx") == 0
    final_device = lax.axis_index("gx") == streamwise_parts - 1
    edge_rows = jnp.stack(
        [
            flux_lines[:, 0],
            flux_lines[:, 1],
            flux_lines[:, streamwise - 2],
            flux_lines[:, streamwise - 1],
        ]
    )
    widened = extended(edge_rows, (("gx", 0),), 2)
    delta_first = -(7.0 / 9.0) * widened[1] - 1.0 / 36.0 * widened[0]
    delta_second = -(1.0 / 36.0) * widened[1]
    delta_penult = 1.0 / 36.0 * widened[6]
    delta_end = 7.0 / 9.0 * widened[6] + 1.0 / 36.0 * widened[7]
    complete = (
        local_solution
        + delta_first[:, None] * inverse[:, 0]
        + delta_second[:, None] * inverse[:, 1]
        + delta_penult[:, None] * inverse[:, streamwise - 2]
        + delta_end[:, None] * inverse[:, streamwise - 1]
    )
    end_rows = jnp.stack([complete[:, 0], complete[:, streamwise - 1]])
    neighbour_ends = extended(end_rows, (("gx", 0),), 1)
    preceding = jnp.where(
        first_device, 0.0, (neighbour_ends[0] - third_part * corner * complete[:, 0]) * scale_term
    )
    following = jnp.where(
        final_device,
        0.0,
        (neighbour_ends[3] - third_part * corner * complete[:, streamwise - 1]) * scale_term,
    )
    solution = complete - third_part * (
        preceding[:, None] * inverse[:, 0] + following[:, None] * inverse[:, streamwise - 1]
    )
    derivative = solution.reshape(flux_fields.shape)
    conserved = jnp.concatenate([density[None], momentum, energy[None]], axis=0)
    advanced = conserved - step_size * derivative
    advanced = jnp.concatenate([advanced[0:1], advanced[1:4] * fluid_cells, advanced[4:5]], axis=0)
    widened_rows = extended(advanced, (("gy", 2),), 5)
    weights = filter_weights()
    weighted = weights[0] * advanced
    for distance in range(1, 6):
        weighted = weighted + 0.5 * weights[distance] * (
            widened_rows[:, :, 5 + distance : 5 + distance + transverse]
            + widened_rows[:, :, 5 - distance : 5 - distance + transverse]
        )
    transverse_total = transverse * transverse_parts
    row_place = lax.axis_index("gy") * transverse + jnp.arange(transverse)
    interior = (row_place >= 5) & (row_place <= transverse_total - 6)
    filter_side = jnp.where(interior[None, None, :, None], weighted, advanced)
    coupling = jnp.where(interior, filter_alpha, 0.0).astype(jnp.float32)
    eliminated_upper = jnp.where(interior, eliminated(row_place - 4), 0.0)
    pivots = jnp.where(interior, 1.0 - filter_alpha * eliminated(row_place - 5), 1.0)
    row_values = [filter_side[:, :, offset, :] for offset in range(transverse)]
    offsets = list(range(transverse))
    reversed_offsets = offsets[::-1]
    forward_values, forward_products, forward_end, forward_total = local_pass(
        row_values, -coupling / pivots, pivots, offsets
    )
    incoming = prefix(
        (forward_total, forward_end),
        "gy",
        compose,
        (jnp.ones((), jnp.float32), jnp.zeros_like(forward_end)),
        False,
    )
    from_below = incoming[1]
    eliminated_rows = [
        forward_values[offset] + forward_products[offset] * from_below for offset in offsets
    ]
    ones_column = jnp.ones((transverse,), jnp.float32)
    back_values, back_products, back_end, back_total = local_pass(
        eliminated_rows, -eliminated_upper, ones_column, reversed_offsets
    )
    arriving = prefix(
        (back_total, back_end),
        "gy",
        compose,
        (jnp.ones((), jnp.float32), jnp.zeros_like(back_end)),
        True,
    )
    from_above = arriving[1]
    smoothed = [back_values[offset] + back_products[offset] * from_above for offset in offsets]
    filtered = jnp.stack(smoothed, axis=2)
    return jnp.concatenate([filtered[0:1], filtered[1:4] * fluid_cells, filtered[4:5]], axis=0)


def solution(mesh):
    placed = (
        P(None, "gy", "gx"),
        P(None, None, "gy", "gx"),
        P(None, "gy", "gx"),
        P(None, "gy", "gx"),
    )
    return jax.shard_map(
        body, mesh=mesh, in_specs=placed, out_specs=P(None, None, "gy", "gx"), check_vma=False
    )
```

profile of v0, /device:TPU:6, one launch (start us, length us, event | category | flops | bytes accessed | tf_op | source)
XLA Modules:
  0.0 1736.6 jit_solution(3579383079488443227)
XLA Ops:
  11.8 1.9 collective-permute-start
  14.0 3.6 collective-permute-start.1
  22.5 265.8 %while.96 = (s32[]{:T(128)}, f32[]{:T(128)}, f32[1]{0:T(128)}, f32[3,32]{1,0:T(4,128)S(1)}, f32[3,32,1]{1,2,0:T(1,128)S(1)}, /*index=5*/f32[3,32]{1,0:T(4,128)S(...) while((s32[]{:T(128)}, f32[]{:T(128)}, f32[1]{0:T(128)}, ...), condition=%wide.region_5.6_spmd, body=%wide.region_4.5_spmd.sunk | while | flops 194 | bytes 5757 | solution.py:142
  296.0 194.7 %while.94 = (s32[]{:T(128)}, f32[]{:T(128)}, f32[128]{0:T(128)S(1)}, f32[3,32]{1,0:T(4,128)S(1)}, f32[3,32,128]{2,1,0:T(8,128)S(1)}, /*index=5*/f32[3,32]{1,0:T(...) while((s32[]{:T(128)}, f32[]{:T(128)}, ...), condition=%wide.region_1.2_spmd, body=%wide.region_0.1_spmd.sunk | while | flops 12417 | bytes 103653 | solution.py:139
  338.9 20.0 %fusion.418 = (f32[128]{0:T(128)S(1)}, f32[128]{0:T(128)S(1)}, f32[128]{0:T(128)S(1)}, f32[128]{0:T(128)S(1)}, f32[128]{0:T(128)S(1)}, /*index=5*/f32[128]{0:T(1...) fusion(f32[3,32,128]{2,1,0:T(8,128)S(1)} %get-tuple-element.242, ...), kind=kLoop, calls=%fused_computation.40.clone.1 | loop fusion | flops 12288 | bytes 33664 | tf_op jit(solution)/shard_map/while/body/eval_jaxpr/div | solution.py:139
  403.8 20.0 %fusion.418 = (f32[128]{0:T(128)S(1)}, f32[128]{0:T(128)S(1)}, f32[128]{0:T(128)S(1)}, f32[128]{0:T(128)S(1)}, f32[128]{0:T(128)S(1)}, /*index=5*/f32[128]{0:T(1...) fusion(f32[3,32,128]{2,1,0:T(8,128)S(1)} %get-tuple-element.242, ...), kind=kLoop, calls=%fused_computation.40.clone.1 | loop fusion | flops 12288 | bytes 33664 | tf_op jit(solution)/shard_map/while/body/eval_jaxpr/div | solution.py:139
  468.6 20.0 %fusion.418 = (f32[128]{0:T(128)S(1)}, f32[128]{0:T(128)S(1)}, f32[128]{0:T(128)S(1)}, f32[128]{0:T(128)S(1)}, f32[128]{0:T(128)S(1)}, /*index=5*/f32[128]{0:T(1...) fusion(f32[3,32,128]{2,1,0:T(8,128)S(1)} %get-tuple-element.242, ...), kind=kLoop, calls=%fused_computation.40.clone.1 | loop fusion | flops 12288 | bytes 33664 | tf_op jit(solution)/shard_map/while/body/eval_jaxpr/div | solution.py:139
  574.0 128.8 %while.97 = (s32[]{:T(128)}, f32[1]{0:T(128)}, f32[3,32,1]{1,2,0:T(1,128)S(1)}, f32[3,32]{1,0:T(4,128)S(1)}, s32[]{:T(128)}, /*index=5*/s32[]{:T(128)}) while((s32[]{:T(128)}, f32[1]{0:T(128)}, f32[3,32,1]{1,2,0:T(1,128)S(1)}, f32[3,32]{1,0:T(4,128)S(1)}, s32[]{:T(128)}, /*index=5*/s32[]{:T(128)}) %tuple.921), condition=%wide.region_7.8_spmd, body=%wide.region_6.7_spmd.sunk | while | flops 67 | bytes 1881 | solution.py:142
  742.6 19.4 %subtract_divide_fusion = (f32[128]{0:T(128)S(1)}, f32[128]{0:T(128)S(1)}, f32[128]{0:T(128)S(1)}, f32[128]{0:T(128)S(1)}, f32[128]{0:T(128)S(1)}, /*index=5*/f3...) fusion(f32[128]{0:T(128)S(1)} %get-tuple-element.639, ...), kind=kLoop, calls=%fused_computation.521 | loop fusion | flops 11904 | bytes 32504 | tf_op jit(solution)/shard_map/eval_jaxpr/div | solution.py:139
  762.1 65.1 %while.95 = (s32[]{:T(128)}, f32[128]{0:T(128)S(1)}, f32[3,32,128]{2,1,0:T(8,128)S(1)}, f32[3,32,128]{2,1,0:T(8,128)S(1)}, f32[3,32]{1,0:T(4,128)S(1)}, /*index=...) while((s32[]{:T(128)}, f32[128]{0:T(128)S(1)}, ...), condition=%wide.region_3.4_spmd, body=%wide.region_2.3_spmd.sunk | while | flops 8226 | bytes 101333 | solution.py:139
  763.5 20.1 %fusion.421 = (f32[128]{0:T(128)S(1)}, f32[128]{0:T(128)S(1)}, f32[128]{0:T(128)S(1)}, f32[128]{0:T(128)S(1)}, f32[128]{0:T(128)S(1)}, /*index=5*/f32[128]{0:T(1...) fusion(f32[3,32,128]{2,1,0:T(8,128)S(1)} %get-tuple-element.253, ...), kind=kLoop, calls=%fused_computation.168.clone.1 | loop fusion | flops 8192 | bytes 33536 | tf_op jit(solution)/shard_map/while/body/eval_jaxpr/sub | solution.py:139
  785.2 20.1 %fusion.421 = (f32[128]{0:T(128)S(1)}, f32[128]{0:T(128)S(1)}, f32[128]{0:T(128)S(1)}, f32[128]{0:T(128)S(1)}, f32[128]{0:T(128)S(1)}, /*index=5*/f32[128]{0:T(1...) fusion(f32[3,32,128]{2,1,0:T(8,128)S(1)} %get-tuple-element.253, ...), kind=kLoop, calls=%fused_computation.168.clone.1 | loop fusion | flops 8192 | bytes 33536 | tf_op jit(solution)/shard_map/while/body/eval_jaxpr/sub | solution.py:139
  806.9 20.1 %fusion.421 = (f32[128]{0:T(128)S(1)}, f32[128]{0:T(128)S(1)}, f32[128]{0:T(128)S(1)}, f32[128]{0:T(128)S(1)}, f32[128]{0:T(128)S(1)}, /*index=5*/f32[128]{0:T(1...) fusion(f32[3,32,128]{2,1,0:T(8,128)S(1)} %get-tuple-element.253, ...), kind=kLoop, calls=%fused_computation.168.clone.1 | loop fusion | flops 8192 | bytes 33536 | tf_op jit(solution)/shard_map/while/body/eval_jaxpr/sub | solution.py:139
  828.4 2.6 fusion.273
  831.0 2.7 fusion.272
  833.7 2.6 fusion.271
  836.3 2.7 fusion.270
  839.0 2.5 fusion.269
  841.5 2.7 fusion.268
  844.2 2.7 fusion.267
  846.9 2.6 fusion.266
  849.5 2.7 fusion.265
  852.2 2.7 fusion.264
  854.8 2.6 fusion.263
  857.4 2.7 fusion.262
  860.1 2.6 fusion.261
  862.7 2.5 fusion.260
  865.3 2.0 fusion.252
  904.2 1.9 collective-permute-start.2
  906.1 3.8 collective-permute-start.3
  921.8 4.9 collective-permute-start.5
  928.1 1.5 collective-permute-done.5
  930.9 19.2 %fusion.205 = f32[1,5,8,128]{3,2,1,0:T(8,128)} fusion(f32[1,5,8,128]{3,2,1,0:T(8,128)S(1)} %bitcast.2823, f32[]{:T(128)} %bitcast.573, f32[]{:T(128)} %bitcast.574, f32[]{:T(128)} %bitcast.575, f32[]{:T(128)} %bitcast.576, f32[]{:T(128)} %bitcast.577, f32[]{:T(128)} %bitcast.578, f32[]{:T(128)} %bitcast.579, f32[]{:T(128)} %bitcast.572, f32[]{:T(128)} %bitcast.571, ...), kind=kLoop, calls=%fused_computation.361 | loop fusion | flops 235520 | bytes 348284 | tf_op jit(solution)/shard_map/add | solution.py:93
  974.5 222.7 %all-reduce.3 = (f32[96]{0:T(128)S(1)}, f32[96]{0:T(128)S(1)}) all-reduce(f32[96]{0:T(128)S(1)} %dynamic-update-slice, f32[96]{0:T(128)S(1)} %dynamic-update-slice.1), channel_id=1, replica_groups=mesh['gx'=8,'gy'=96] {'gy'}, use_global_device_ids=true, to_apply=%add.1 | all-reduce | flops 192 | bytes 1536
  1197.2 188.5 %while.98 = (s32[]{:T(128)}, f32[5,8,128]{2,1,0:T(8,128)S(1)}, s32[]{:T(128)}, f32[96]{0:T(128)S(1)}, f32[96,5,8,128]{3,2,1,0:T(8,128)}, /*index=5*/s32[]{:T(128)}, s32[]{:T(128)}) while((s32[]{:T(128)}, f32[5,8,128]{2,1,0:T(8,128)S(1)}, s32[]{:T(128)}, f32[96]{0:T(128)S(1)}, f32[96,5,8,128]{3,2,1,0:T(8,128)}, ...), condition=%wide.region_9.10_spmd.clone, body=%wide.region_8.9_spmd.clone.sunk | while | flops 20484 | bytes 61557 | solution.py:42
  1197.8 1.4 fusion.432
  1199.8 1.4 fusion.432
  1201.7 1.4 fusion.432
  1203.7 1.4 fusion.432
  1205.7 1.4 fusion.432
  1207.6 1.4 fusion.432
  1209.6 1.4 fusion.432
  1211.5 1.4 fusion.432
  1213.5 1.4 fusion.432
  1215.5 1.4 fusion.432
  1385.7 29.5 %fusion.212 = (f32[5,8,128]{2,1,0:T(8,128)}, f32[5,8,128]{2,1,0:T(8,128)S(1)}, f32[5,8,128]{2,1,0:T(8,128)S(1)}, f32[5,8,128]{2,1,0:T(8,128)S(1)}, f32[5,8,128]{...) fusion(f32[5,8,128]{2,1,0:T(8,128)S(1)} %get-tuple-element.533,, ...), kind=kLoop, calls=%fused_computation.391 | loop fusion | flops 558080 | bytes 655612 | tf_op jit(solution)/shard_map/add | solution.py:93
  1415.2 118.1 %all-gather.6.cloned.1.call-done = f32[480,8,128]{2,1,0:T(8,128)} async-done(((f32[5,8,128]{2,1,0:T(8,128)}), f32[480,8,128]{2,1,0:T(8,128)}) %all-gather.6.cloned.1.call-update) | async-done | bytes 1966096 | tf_op jit(solution)/shard_map/all_gather | solution.py:29
  1533.4 188.2 %while.99 = (s32[]{:T(128)}, f32[5,8,128]{2,1,0:T(8,128)S(1)}, s32[]{:T(128)}, f32[96]{0:T(128)S(1)}, f32[96,5,8,128]{3,2,1,0:T(8,128)}, /*index=5*/s32[]{:T(128)}, s32[]{:T(128)}, s32[]{:T(128)}, s32[]{:T(128)}) while((s32[]{:T(128)}, f32[5,8,128]{2,1,0:T(8,128)S(1)}, s32[]{:T(128)}, f32[96]{0:T(128)S(1)}, ...), condition=%wide.region_11.12_spmd.clone, body=%wide.region_10.11_spmd.clone.sunk | while | flops 20488 | bytes 61619 | solution.py:42
  (654 shorter events, 452.0 us)
Async XLA Ops:
  6.5 1190.7 %all-gather.4.cloned.1.call-start = ((), (), s32[]{:S(2)}) async-start(), calls=%async_computation | async-start | bytes 1986560 | tf_op jit(solution)/shard_map/all_gather | solution.py:29
  11.8 891.1 %collective-permute-start = (f32[2,640]{1,0:T(2,128)S(1)}, f32[2,640]{1,0:T(2,128)S(1)}, u32[]{:S(2)}, u32[]{:S(2)}) collective-permute-start(f32[2,640]{1,0:T(2,128)S(1)} %pad_maximum_fusion.3), channel_id=1, source_target_pairs={{0,96},{96,192},{192,288},{288,384},{384,480},{480,576},{576,672},... | collective-permute-start | bytes 15368 | tf_op jit(solution)/shard_map/ppermute | solution.py:21
  14.0 888.9 %collective-permute-start.1 = (f32[2,640]{1,0:T(2,128)S(1)}, f32[2,640]{1,0:T(2,128)S(1)}, u32[]{:S(2)}, u32[]{:S(2)}) collective-permute-start(f32[2,640]{1,0:T(2,128)S(1)} %pad_maximum_fusion.4), channel_id=1, source_target_pairs={{96,0},{192,96},{288,192},{384,288},{480,384},{576,480},{672,576},... | collective-permute-start | bytes 15368 | tf_op jit(solution)/shard_map/ppermute | solution.py:22
  490.7 336.5 %copy-start.2 = (f32[3,32,128]{2,1,0:T(8,128)}, f32[3,32,128]{2,1,0:T(8,128)S(1)}, u32[]{:S(2)}) copy-start(f32[3,32,128]{2,1,0:T(8,128)S(1)} %get-tuple-element.522) | copy-start | bytes 147460
  869.3 2.8 copy-start.4
  873.0 47.4 %copy-start = (f32[3,8,16,128]{3,2,1,0:T(8,128)S(1)}, f32[3,8,16,128]{3,2,1,0:T(8,128)}, u32[]{:S(2)}) copy-start(f32[3,8,16,128]{3,2,1,0:T(8,128)} %param.17) | copy-start | bytes 589828
  873.0 47.4 %copy-start.1 = (f32[8,16,128]{2,1,0:T(8,128)S(1)}, f32[8,16,128]{2,1,0:T(8,128)}, u32[]{:S(2)}) copy-start(f32[8,16,128]{2,1,0:T(8,128)} %param.18) | copy-start | bytes 196612
  873.0 47.4 %copy-start.3 = (f32[8,16,128]{2,1,0:T(8,128)S(1)}, f32[8,16,128]{2,1,0:T(8,128)}, u32[]{:S(2)}) copy-start(f32[8,16,128]{2,1,0:T(8,128)} %param.16) | copy-start | bytes 196612
  904.2 15.7 collective-permute-start.2
  906.1 13.8 collective-permute-start.3
  920.5 7.6 collective-permute-start.4
  921.8 7.7 collective-permute-start.5
  950.2 583.2 %all-gather.6.cloned.1.call-start = ((), (), s32[]{:S(2)}) async-start(), calls=%async_computation.1 | async-start | bytes 1986560 | tf_op jit(solution)/shard_map/all_gather | solution.py:29
Sparse Core Ops, SparseCore 0:
  950.3 132.8 all-gather.3
  1415.3 118.0 all-gather.5
where the time goes:
time: 1760 us; the launch traced here: 1740 us
  other arithmetic  503 us (29%)
  loops' own time  492 us (28%)
  blocking collectives  223 us (13%)
  between operations  193 us (11%)
  local copies, waits for them, and re-layouts  186 us (11%)
  waiting for transfers between devices  121 us (7%)
  starting transfers between devices  17.6 us (1%)
    another operation x2, loops' own time, body(): lax.linalg.tridiagonal_solve(plain_lower, diagonal, plain_upper, identity...  369 us
    select_n x192, other arithmetic, step(): return jax.tree.map(lambda a, b: jnp.where(reached, a, b), new, before)  262 us
    unnamed x1, blocking collectives  223 us
    another operation x2, loops' own time, body(): lax.linalg.tridiagonal_solve(lower_band, diagonal, upper_band, identity)  123 us
    all_gather x2, waiting for transfers between devices, prefix(): everything = jax.tree.map(lambda part: lax.all_gather(part, axis), shard)  118 us
    dynamic_slice x192, local copies, waits for them, and re-layouts, step(): new = combine(before, jax.tree.map(lambda part: part[at], everything))  115 us
    div x4, other arithmetic, body(): lax.linalg.tridiagonal_solve(lower_band, diagonal, upper_band, identity)  79.4 us
    sub x3, other arithmetic, body(): lax.linalg.tridiagonal_solve(lower_band, diagonal, upper_band, identity)  60.3 us
  transfers between devices with their start and end apart: 8, of which 3 were waited for; matrix products, arithmetic and copies ran while one was open for 14% of the time, Pallas kernels for 0%

commit v1 on v0

v1 whole, which is shorter than its diff:
```python
import functools
import math

import jax
import jax.numpy as jnp
import numpy as np
from jax import lax
from jax.experimental import pallas as pl
from jax.experimental.pallas import tpu as pltpu
from jax.sharding import PartitionSpec as P

gas_gamma = 1.4
step_size = 0.1
filter_alpha = 0.4999
reach = 5
inner = 12
exact = lax.Precision.HIGHEST


def derivative_matrix(length):
    left = np.eye(length)
    right = np.zeros((length, length))
    for i in range(2, length - 2):
        left[i, i - 1] = left[i, i + 1] = 1.0 / 3.0
        right[i, i + 1], right[i, i - 1] = 7.0 / 9.0, -7.0 / 9.0
        right[i, i + 2], right[i, i - 2] = 1.0 / 36.0, -1.0 / 36.0
    left[0, 1] = 2.0
    right[0, :3] = -2.5, 2.0, 0.5
    left[1, 0] = left[1, 2] = 0.25
    right[1, 0], right[1, 2] = -0.75, 0.75
    left[-2, -3] = left[-2, -1] = 0.25
    right[-2, -3], right[-2, -1] = -0.75, 0.75
    left[-1, -2] = 2.0
    right[-1, -3:] = -0.5, -2.0, 2.5
    return np.linalg.solve(left, right)


def streamwise_tables(parts, width):
    whole = derivative_matrix(parts * width)
    rows = [slice(p * width, (p + 1) * width) for p in range(parts)]
    own = np.stack([whole[rows[p], rows[p]].T for p in range(parts)])
    sends = np.zeros((parts, 8, width))
    applied = np.zeros((parts, 8, width))
    for p in range(parts):
        if p + 1 < parts:
            block = whole[rows[p + 1], rows[p]]
            sends[p, 0:2] = block[0:2]
            applied[p + 1, 0, 0] = 1.0
            applied[p + 1, 1, 1:] = block[1:, -1] / block[1, -1]
        if p > 0:
            block = whole[rows[p - 1], rows[p]]
            sends[p, 2], sends[p, 3] = block[-1], block[-2]
            applied[p - 1, 2, -1] = 1.0
            applied[p - 1, 3, :-1] = block[:-1, 0] / block[-2, 0]
    return (
        (-step_size * own).astype(np.float32),
        sends.astype(np.float32),
        (-step_size * applied).astype(np.float32),
    )


def correction_matrix(length):
    count = length - 2 * reach
    left = np.eye(count)
    index = np.arange(count - 1)
    left[index, index + 1] = left[index + 1, index] = filter_alpha
    right = np.zeros((count, length))
    scale = (1.0 - 2.0 * filter_alpha) / 1024.0
    for shift in range(-reach, reach + 1):
        right[np.arange(count), np.arange(count) + reach + shift] = (
            scale * (-1.0) ** shift * math.comb(10, reach + shift)
        )
    whole = np.zeros((length, length))
    whole[reach : length - reach] = np.linalg.solve(left, right)
    return whole


def transverse_tables(parts, width):
    length = parts * width
    whole = correction_matrix(length)
    eta = math.acosh(0.5 / filter_alpha)

    def falling(ahead, behind):
        last = length - reach
        sign = (-1.0) ** (ahead - behind)
        return sign * math.sinh((last - ahead) * eta) / math.sinh((last - behind) * eta)

    def rising(ahead, behind):
        sign = (-1.0) ** (ahead - behind)
        return sign * math.sinh((ahead - reach + 1) * eta) / math.sinh((behind - reach + 1) * eta)

    outer = parts // inner
    own = np.zeros((parts, width, width + 2 * reach))
    up = np.zeros((parts, width))
    down = np.zeros((parts, width))
    from_low = np.zeros((parts, width))
    from_high = np.zeros((parts, width))
    for p in range(parts):
        start, end = p * width, (p + 1) * width - 1
        cells = slice(start, end + 1)
        if p + 1 < parts:
            up[p] = whole[end + 1 + reach, cells] * falling(end + 1, end + 1 + reach)
        if p > 0:
            down[p] = whole[start - 1 - reach, cells] * rising(start - 1, start - 1 - reach)
        for row in range(start, end + 1):
            if reach <= row < length - reach:
                from_low[p, row - start] = falling(row, start)
                from_high[p, row - start] = rising(row, end)
    for p in range(parts):
        start, end = p * width, (p + 1) * width - 1
        cells = slice(start, end + 1)
        own[p, :, reach : reach + width] = whole[cells, cells]
        if p > 0:
            near = whole[cells, start - reach : start]
            own[p, :, :reach] = near - np.outer(from_low[p], up[p - 1, -reach:])
        if p + 1 < parts:
            near = whole[cells, end + 1 : end + 1 + reach]
            own[p, :, reach + width :] = near - np.outer(from_high[p], down[p + 1, :reach])
    within = np.zeros((parts, 4, inner))
    across = np.zeros((parts, 2, outer))
    for p in range(parts):
        group, place = divmod(p, inner)
        start, end = p * width, (p + 1) * width - 1
        low_edge, high_edge = group * inner * width - 1, (group + 1) * inner * width
        for k in range(inner):
            q = group * inner + k
            if k < place:
                within[p, 0, k] = falling(start, (q + 1) * width)
            if k > place:
                within[p, 1, k] = rising(end, q * width - 1)
            if group + 1 < outer:
                within[p, 2, k] = falling(high_edge, (q + 1) * width)
            if group > 0:
                within[p, 3, k] = rising(low_edge, q * width - 1)
        for other in range(outer):
            if other < group:
                across[p, 0, other] = falling(start, (other + 1) * inner * width)
            if other > group:
                across[p, 1, other] = rising(end, other * inner * width - 1)
    ends = np.stack([up, down], axis=1)
    last = np.concatenate(
        [
            own.reshape(parts, -1),
            from_low,
            from_high,
            across.reshape(parts, -1),
        ],
        axis=1,
    )
    return [packed(table) for table in (ends, within, last)]


def packed(table):
    parts = table.shape[0]
    flat = table.reshape(parts, -1)
    room = -(-flat.shape[1] // 128) * 128
    wide = np.zeros((parts, 1, room), np.float32)
    wide[:, 0, : flat.shape[1]] = flat
    return wide


def first_kernel(place, density, momentum, energy, flags, own, sends, partial, fluid, to_right, to_left, flux):
    planes, transverse = 8, 16
    cells = planes * transverse
    for j in range(transverse):
        picked = pl.ds(j, planes, stride=transverse)
        rho = density[picked, :]
        m0 = momentum[pl.ds(j, planes, stride=transverse), :]
        m1 = momentum[pl.ds(cells + j, planes, stride=transverse), :]
        m2 = momentum[pl.ds(2 * cells + j, planes, stride=transverse), :]
        total = energy[picked, :]
        row = pl.ds(j * planes, planes)
        fluid[row, :] = (1 - flags[picked, :]).astype(jnp.float32)
        inverse = 1.0 / rho
        velocity = m0 * inverse
        kinetic = 0.5 * (m0 * m0 + m1 * m1 + m2 * m2) * inverse
        pressure = (gas_gamma - 1.0) * (total - kinetic)
        fields = (
            m0,
            m0 * velocity + pressure,
            m1 * velocity,
            m2 * velocity,
            (total + pressure) * velocity,
        )
        for f, (held, moved) in enumerate(zip((rho, m0, m1, m2, total), fields)):
            at = pl.ds(f * cells + j * planes, planes)
            partial[at, :] = held
            flux[at, :] = moved
    lines = flux[...]
    sent = lax.dot_general(
        sends[0], lines, (((1,), (1,)), ((), ())), precision=exact, preferred_element_type=jnp.float32
    )
    to_right[...] = sent[0:2]
    to_left[...] = sent[2:4]
    partial[...] = partial[...] + jnp.dot(
        lines, own[0], precision=exact, preferred_element_type=jnp.float32
    )


def second_kernel(place, partial, fluid, before, after, applied, ends, advanced, summed, upper, lower):
    planes, transverse = 8, 16
    cells = planes * transverse
    count = partial.shape[0]
    received = jnp.concatenate(
        [before[...], after[...], jnp.zeros((4, count), jnp.float32)], axis=0
    )
    added = lax.dot_general(
        received, applied[0], (((0,), (0,)), ((), ())), precision=exact, preferred_element_type=jnp.float32
    )
    state = partial[...] + added
    mask = fluid[...]
    for f in range(5):
        part = state[f * cells : (f + 1) * cells]
        if 1 <= f <= 3:
            part = part * mask
        advanced[f * cells : (f + 1) * cells, :] = part
        low, high = None, None
        for j in range(transverse):
            row = part[j * planes : (j + 1) * planes]
            one, two = ends[0, 0, j] * row, ends[0, 0, transverse + j] * row
            low = one if low is None else low + one
            high = two if high is None else high + two
        summed[f * planes : (f + 1) * planes, :] = low
        summed[(5 + f) * planes : (6 + f) * planes, :] = high
        width = reach * planes
        upper[f * width : (f + 1) * width, :] = part[cells - width :]
        lower[f * width : (f + 1) * width, :] = part[:width]


def third_kernel(place, gathered, within, prefix, slab):
    lines = gathered.shape[1] // 2
    outer = slab.shape[0]
    group = place[1]
    sums = []
    for kind in range(4):
        side = kind % 2
        total = None
        for k in range(inner):
            term = within[0, 0, kind * inner + k] * gathered[k, side * lines : (side + 1) * lines, :]
            total = term if total is None else total + term
        sums.append(total)
    prefix[:lines, :] = sums[0]
    prefix[lines:, :] = sums[1]
    for other in range(outer):
        slab[other, :, :] = jnp.where(other > group, sums[2], sums[3])


def last_kernel(place, advanced, fluid, before, after, prefix, exchanged, table, result):
    planes, transverse = 8, 16
    cells = planes * transverse
    lines = 5 * planes
    outer = exchanged.shape[0]
    span = transverse + 2 * reach
    base = transverse * span
    low, high = prefix[:lines, :], prefix[lines:, :]
    for other in range(outer):
        low = low + table[0, 0, base + 2 * transverse + other] * exchanged[other]
        high = high + table[0, 0, base + 2 * transverse + outer + other] * exchanged[other]
    width = reach * planes

    def cell(f, k):
        if k < reach:
            return before[f * width + k * planes : f * width + (k + 1) * planes, :]
        k -= reach
        if k < transverse:
            return advanced[f * cells + k * planes : f * cells + (k + 1) * planes, :]
        k -= transverse
        return after[f * width + k * planes : f * width + (k + 1) * planes, :]

    for i in range(transverse):
        falls, rises = table[0, 0, base + i], table[0, 0, base + transverse + i]
        sums = [
            falls * low[f * planes : (f + 1) * planes] + rises * high[f * planes : (f + 1) * planes]
            for f in range(5)
        ]
        for k in range(span):
            if k < reach and i >= reach or k >= reach + transverse and i < transverse - reach:
                continue
            weight = table[0, 0, i * span + k]
            sums = [total + weight * cell(f, k) for f, total in enumerate(sums)]
        keep = fluid[i * planes : (i + 1) * planes, :]
        for f in range(5):
            value = cell(f, reach + i) - sums[f]
            if 1 <= f <= 3:
                value = value * keep
            result[pl.ds(f * cells + i, planes, stride=transverse), :] = value


def whole_block(shape):
    return pl.BlockSpec(shape, lambda i, place: (0,) * len(shape))


def picked_block(table, which, space=None):
    zeros = (0,) * (table.ndim - 1)
    shape = (1,) + table.shape[1:]
    if space is None:
        return pl.BlockSpec(shape, lambda i, place: (place[which],) + zeros)
    return pl.BlockSpec(shape, lambda i, place: (place[which],) + zeros, memory_space=space)


def call(kernel, name, place, arrays, tables, outs, scratch=()):
    in_specs = [whole_block(a.shape) for a in arrays]
    in_specs += [picked_block(table, which, space) for table, which, space in tables]
    shapes = [jax.ShapeDtypeStruct(shape, jnp.float32) for shape in outs]
    return pl.pallas_call(
        kernel,
        grid_spec=pltpu.PrefetchScalarGridSpec(
            num_scalar_prefetch=1,
            grid=(1,),
            in_specs=in_specs,
            out_specs=[whole_block(shape) for shape in outs],
            scratch_shapes=list(scratch),
        ),
        out_shape=shapes,
        name=name,
    )(place, *arrays, *[jnp.asarray(table) for table, _, _ in tables])


def body(tables, density, momentum, energy, solid_flags):
    own, sends, applied, ends, within, last = tables
    planes, transverse, width = density.shape
    cells = planes * transverse
    parts, columns = lax.axis_size("gy"), lax.axis_size("gx")
    outer = parts // inner
    gx, gy = lax.axis_index("gx"), lax.axis_index("gy")
    place = jnp.stack([gy, gy // inner, gx]).astype(jnp.int32)
    smem = pltpu.SMEM
    partial, fluid, to_right, to_left = call(
        first_kernel,
        "flux_step",
        place,
        [
            density.reshape(cells, width),
            momentum.reshape(3 * cells, width),
            energy.reshape(cells, width),
            solid_flags.reshape(cells, width),
        ],
        [(own, 2, None), (sends, 2, None)],
        [(5 * cells, width), (cells, width), (2, 5 * cells), (2, 5 * cells)],
        [pltpu.VMEM((5 * cells, width), jnp.float32)],
    )
    up = [(i, i + 1) for i in range(columns - 1)]
    down = [(i + 1, i) for i in range(columns - 1)]
    before = lax.ppermute(to_right, "gx", up)
    after = lax.ppermute(to_left, "gx", down)
    lines = 5 * planes
    advanced, summed, upper, lower = call(
        second_kernel,
        "advance_step",
        place,
        [partial, fluid, before, after],
        [(applied, 2, None), (ends, 0, smem)],
        [
            (5 * cells, width),
            (2 * lines, width),
            (reach * lines, width),
            (reach * lines, width),
        ],
    )
    low_rows = lax.ppermute(upper, "gy", [(i, i + 1) for i in range(parts - 1)])
    high_rows = lax.ppermute(lower, "gy", [(i + 1, i) for i in range(parts - 1)])
    near = [[g * inner + k for k in range(inner)] for g in range(outer)]
    far = [[g * inner + k for g in range(outer)] for k in range(inner)]
    gathered = lax.all_to_all(
        jnp.broadcast_to(summed[None], (inner, 2 * lines, width)),
        "gy",
        0,
        0,
        axis_index_groups=near,
    )
    prefix, slab = call(
        third_kernel,
        "group_step",
        place,
        [gathered],
        [(within, 0, smem)],
        [(2 * lines, width), (outer, lines, width)],
    )
    exchanged = lax.all_to_all(slab, "gy", 0, 0, axis_index_groups=far)
    (result,) = call(
        last_kernel,
        "filter_step",
        place,
        [advanced, fluid, low_rows, high_rows, prefix, exchanged],
        [(last, 0, smem)],
        [(5 * cells, width)],
    )
    return result.reshape(5, planes, transverse, width)


def solution(mesh):
    columns, parts = mesh.shape["gx"], mesh.shape["gy"]
    tables = streamwise_tables(columns, 1024 // columns) + tuple(
        transverse_tables(parts, 1536 // parts)
    )
    placed = (
        P(None, "gy", "gx"),
        P(None, None, "gy", "gx"),
        P(None, "gy", "gx"),
        P(None, "gy", "gx"),
    )
    return jax.shard_map(
        functools.partial(body, tables),
        mesh=mesh,
        in_specs=placed,
        out_specs=P(None, None, "gy", "gx"),
        check_vma=False,
    )
```

time: 1760 us -> 81.1 us (0.05)
  the two profiles are of different devices: /device:TPU:6 before, /device:TPU:36 now
where the time goes in v1:
time: 81.1 us; the launch traced here: 80.5 us
  blocking collectives  40.1 us (49%)
  starting transfers between devices  22 us (27%)
  Pallas kernels  11.8 us (15%)
  waiting for transfers between devices  3.74 us (5%)
  local copies, waits for them, and re-layouts  2.1 us (3%)
    all_to_all x1, blocking collectives, body(): lax.all_to_all(jnp.broadcast_to(summed[None], (inner, 2 * lines, width)),...  40.1 us
    pallas_call x4, Pallas kernels, call(): pl.pallas_call(kernel, grid_spec=pltpu.PrefetchScalarGridSpec(num_scalar_...  11.8 us
    all_to_all x1, starting transfers between devices, body(): exchanged = lax.all_to_all(slab, 'gy', 0, 0, axis_index_groups=far)  7.34 us
    ppermute x1, starting transfers between devices, body(): lax.ppermute(lower, 'gy', [(i + 1, i) for i in range(parts - 1)])  5.92 us
    ppermute x1, starting transfers between devices, body(): after = lax.ppermute(to_left, 'gx', down)  3.64 us
    ppermute x1, starting transfers between devices, body(): low_rows = lax.ppermute(upper, 'gy', [(i, i + 1) for i in range(parts - 1)])  3.23 us
    ppermute x1, starting transfers between devices, body(): before = lax.ppermute(to_right, 'gx', up)  1.91 us
  transfers between devices with their start and end apart: 5, of which 3 were waited for; matrix products, arithmetic and copies ran while one was open for 0% of the time, Pallas kernels for 0%

profile of v1, /device:TPU:36, one launch (start us, length us, event | category | flops | bytes accessed | tf_op | source)
XLA Modules:
  0.0 80.5 jit_solution(3246428101307701837)
XLA Ops:
  0.0 0.6 pad_add_fusion.place
  0.7 3.2 %flux_step.1 = (f32[640,128]{1,0:T(8,128)}, f32[128,128]{1,0:T(8,128)}, f32[2,640]{1,0:T(2,128)}, f32[2,640]{1,0:T(2,128)}) custom-call(s32[3]{0:T(128)} %pad_add_fusion.place, f32[128,128]{1,0:T(8,128)} %bitcast.9, f32[384,128]{1,0:T(8,128)} %bitcast.8, f32[128,128]{1,0:T(8,128)} %bitcast.10, s32[128,128]{1,0:T(8,128)} %bitcast.11, ...), custom_call_target="tpu_custom_call" | custom-call | tf_op jit(solution)/shard_map/flux_step/pallas_call | solution.py:305
  3.9 1.9 %collective-permute-start = (f32[2,640]{1,0:T(2,128)}, f32[2,640]{1,0:T(2,128)S(1)}, u32[]{:S(2)}, u32[]{:S(2)}) collective-permute-start(f32[2,640]{1,0:T(2,128)} %get-tuple-element.17), channel_id=1, source_target_pairs={{0,96},{96,192},{192,288},{288,384},{384,480},{480,576},{576,672},... | collective-permute-start | bytes 15368 | tf_op jit(solution)/shard_map/ppermute | solution.py:344
  5.8 3.6 %collective-permute-start.1 = (f32[2,640]{1,0:T(2,128)}, f32[2,640]{1,0:T(2,128)S(1)}, u32[]{:S(2)}, u32[]{:S(2)}) collective-permute-start(f32[2,640]{1,0:T(2,128)} %get-tuple-element.18), channel_id=1, source_target_pairs={{96,0},{192,96},{288,192},{384,288},{480,384},{576,480},{672,576},... | collective-permute-start | bytes 15368 | tf_op jit(solution)/shard_map/ppermute | solution.py:345
  9.4 0.0 collective-permute-done.before
  9.5 0.0 copy-start.3
  9.5 1.5 %collective-permute-done.1.after = f32[2,640]{1,0:T(2,128)S(1)} collective-permute-done((f32[2,640]{1,0:T(2,128)}, f32[2,640]{1,0:T(2,128)S(1)}, u32[]{:S(2)}, u32[]{:S(2)}) %collective-permute-start.1) | collective-permute-done | bytes 5152 | tf_op jit(solution)/shard_map/ppermute | solution.py:345
  11.0 0.0 copy-start.4
  11.0 0.0 copy-done.3
  11.0 0.6 copy-done.4
  11.6 3.0 %advance_step.1 = (f32[640,128]{1,0:T(8,128)}, f32[80,128]{1,0:T(8,128)}, f32[200,128]{1,0:T(8,128)}, f32[200,128]{1,0:T(8,128)}) custom-call(s32[3]{0:T(128)} %pad_add_fusion.place, f32[640,128]{1,0:T(8,128)} %get-tuple-element.15.partial, f32[128,128]{1,0:T(8,128)} %get-tuple-element.16.fluid, f32[2,640]{1,0:T(2,128)} %copy-done.3, f32[2,640]{1,0:T(2,128)} %copy-done.4, ...), custom_call_target="tpu_custom_call" | custom-call | tf_op jit(solution)/shard_map/advance_step/pallas_call | solution.py:305
  14.5 0.8 %broadcast_in_dim.2 = f32[12,80,128]{2,1,0:T(8,128)S(1)} broadcast(f32[80,128]{1,0:T(8,128)} %get-tuple-element.22), dimensions={1,2} | broadcast | bytes 532480 | tf_op jit(solution)/shard_map/broadcast_in_dim | solution.py:365
  15.4 40.1 %all_to_all.10.gathered = f32[12,80,128]{2,1,0:T(8,128)} all-to-all(f32[12,80,128]{2,1,0:T(8,128)S(1)} %broadcast_in_dim.2), channel_id=1, replica_groups={{0,1,2,3,4,5,6,7,8,9,10,11},{12,13,14,15,16,17,18,19,20,21,22,23},{24,2..., dimensions={0} | all-to-all | bytes 983040 | tf_op jit(solution)/shard_map/all_to_all | solution.py:364
  55.5 2.5 %group_step.1 = (f32[80,128]{1,0:T(8,128)}, f32[8,40,128]{2,1,0:T(8,128)}) custom-call(s32[3]{0:T(128)} %pad_add_fusion.place, f32[12,80,128]{2,1,0:T(8,128)} %all_to_all.10.gathered, f32[96,1,128]{2,1,0:T(1,128)} %constant.33.clone.within), custom_call_target="tpu_custom_call" | custom-call | tf_op jit(solution)/shard_map/group_step/pallas_call | solution.py:305
  57.9 0.0 copy-start.6
  57.9 0.0 copy-start.5
  57.9 7.3 %all-to-all-start.1 = ((f32[8,40,128]{2,1,0:T(8,128)}), f32[8,40,128]{2,1,0:T(8,128)S(1)}, u32[]{:S(2)}, u32[]{:S(2)}) async-start(f32[8,40,128]{2,1,0:T(8,128)} %get-tuple-element.24), calls=%async_computation.1 | async-start | bytes 327680 | tf_op jit(solution)/shard_map/all_to_all | solution.py:379
  65.3 0.0 copy-done.6
  65.3 3.2 %collective-permute-start.2 = (f32[200,128]{1,0:T(8,128)S(1)}, f32[200,128]{1,0:T(8,128)S(1)}, u32[]{:S(2)}, u32[]{:S(2)}) collective-permute-start(f32[200,128]{1,0:T(8,128)S(1)} %copy-done.6), channel_id=1, source_target_pairs={{0,1},{1,2},{2,3},{3,4},{4,5},{5,6},{6,7},{7,8},{8,9},{9,10},{10,1... | collective-permute-start | bytes 307208 | tf_op jit(solution)/shard_map/ppermute | solution.py:360
  68.5 0.0 copy-done.5
  68.5 5.9 %collective-permute-start.3 = (f32[200,128]{1,0:T(8,128)S(1)}, f32[200,128]{1,0:T(8,128)S(1)}, u32[]{:S(2)}, u32[]{:S(2)}) collective-permute-start(f32[200,128]{1,0:T(8,128)S(1)} %copy-done.5), channel_id=1, source_target_pairs={{1,0},{2,1},{3,2},{4,3},{5,4},{6,5},{7,6},{8,7},{9,8},{10,9},{11,1... | collective-permute-start | bytes 307208 | tf_op jit(solution)/shard_map/ppermute | solution.py:361
  74.5 0.7 collective-permute-done.2.before
  75.1 0.0 copy-start.1
  75.1 1.5 %collective-permute-done.3.after = f32[200,128]{1,0:T(8,128)S(1)} collective-permute-done((f32[200,128]{1,0:T(8,128)S(1)}, f32[200,128]{1,0:T(8,128)S(1)}, u32[]{:S(2)}, u32[]{:S(2)}) %collective-permute-start.3) | collective-permute-done | bytes 102432 | tf_op jit(solution)/shard_map/ppermute | solution.py:361
  76.7 0.0 copy-start.2
  76.7 0.0 all-to-all-done.1.exchanged
  76.7 0.0 copy-start
  76.7 0.0 copy-done.1
  76.7 0.6 copy-done.2
  77.3 0.1 copy-done
  77.4 3.2 %filter_step.1 = f32[640,128]{1,0:T(8,128)} custom-call(s32[3]{0:T(128)} %pad_add_fusion.place, f32[640,128]{1,0:T(8,128)} %get-tuple-element.19.advanced, f32[128,128]{1,0:T(8,128)} %get-tuple-element.16.fluid, f32[200,128]{1,0:T(8,128)} %copy-done.1, f32[200,128]{1,0:T(8,128)} %copy-done.2, f32[80,128]{1,0:T(8,128)} %get-tuple-element.23.prefix, ...), custom_call_target="tpu_custom_call" | custom-call | tf_op jit(solution)/shard_map/filter_step/pallas_call | solution.py:305
Async XLA Ops:
  3.9 5.6 %collective-permute-start = (f32[2,640]{1,0:T(2,128)}, f32[2,640]{1,0:T(2,128)S(1)}, u32[]{:S(2)}, u32[]{:S(2)}) collective-permute-start(f32[2,640]{1,0:T(2,128)} %get-tuple-element.17), channel_id=1, source_target_pairs={{0,96},{96,192},{192,288},{288,384},{384,480},{480,576},{576,672},... | collective-permute-start | bytes 15368 | tf_op jit(solution)/shard_map/ppermute | solution.py:344
  5.8 5.2 %collective-permute-start.1 = (f32[2,640]{1,0:T(2,128)}, f32[2,640]{1,0:T(2,128)S(1)}, u32[]{:S(2)}, u32[]{:S(2)}) collective-permute-start(f32[2,640]{1,0:T(2,128)} %get-tuple-element.18), channel_id=1, source_target_pairs={{96,0},{192,96},{288,192},{384,288},{480,384},{576,480},{672,576},... | collective-permute-start | bytes 15368 | tf_op jit(solution)/shard_map/ppermute | solution.py:345
  9.5 1.5 %copy-start.3 = (f32[2,640]{1,0:T(2,128)}, f32[2,640]{1,0:T(2,128)S(1)}, u32[]{:S(2)}) copy-start(f32[2,640]{1,0:T(2,128)S(1)} %collective-permute-done.before) | copy-start | bytes 15364
  11.0 0.6 copy-start.4
  57.9 7.3 %copy-start.6 = (f32[200,128]{1,0:T(8,128)S(1)}, f32[200,128]{1,0:T(8,128)}, u32[]{:S(2)}) copy-start(f32[200,128]{1,0:T(8,128)} %get-tuple-element.20) | copy-start | bytes 307204
  57.9 10.6 %copy-start.5 = (f32[200,128]{1,0:T(8,128)S(1)}, f32[200,128]{1,0:T(8,128)}, u32[]{:S(2)}) copy-start(f32[200,128]{1,0:T(8,128)} %get-tuple-element.21) | copy-start | bytes 307204
  57.9 18.8 %all-to-all-start.1 = ((f32[8,40,128]{2,1,0:T(8,128)}), f32[8,40,128]{2,1,0:T(8,128)S(1)}, u32[]{:S(2)}, u32[]{:S(2)}) async-start(f32[8,40,128]{2,1,0:T(8,128)} %get-tuple-element.24), calls=%async_computation.1 | async-start | bytes 327680 | tf_op jit(solution)/shard_map/all_to_all | solution.py:379
  65.3 9.9 %collective-permute-start.2 = (f32[200,128]{1,0:T(8,128)S(1)}, f32[200,128]{1,0:T(8,128)S(1)}, u32[]{:S(2)}, u32[]{:S(2)}) collective-permute-start(f32[200,128]{1,0:T(8,128)S(1)} %copy-done.6), channel_id=1, source_target_pairs={{0,1},{1,2},{2,3},{3,4},{4,5},{5,6},{6,7},{7,8},{8,9},{9,10},{10,1... | collective-permute-start | bytes 307208 | tf_op jit(solution)/shard_map/ppermute | solution.py:360
  68.5 8.2 %collective-permute-start.3 = (f32[200,128]{1,0:T(8,128)S(1)}, f32[200,128]{1,0:T(8,128)S(1)}, u32[]{:S(2)}, u32[]{:S(2)}) collective-permute-start(f32[200,128]{1,0:T(8,128)S(1)} %copy-done.5), channel_id=1, source_target_pairs={{1,0},{2,1},{3,2},{4,3},{5,4},{6,5},{7,6},{8,7},{9,8},{10,9},{11,1... | collective-permute-start | bytes 307208 | tf_op jit(solution)/shard_map/ppermute | solution.py:361
  75.1 1.6 %copy-start.1 = (f32[200,128]{1,0:T(8,128)}, f32[200,128]{1,0:T(8,128)S(1)}, u32[]{:S(2)}) copy-start(f32[200,128]{1,0:T(8,128)S(1)} %collective-permute-done.2.before) | copy-start | bytes 307204
  76.7 0.6 copy-start.2
  76.7 0.7 copy-start

commit v2 on v1

--- a/solution.py
+++ b/solution.py
@@ -159,7 +159,7 @@
     return wide
 
 
-def first_kernel(place, density, momentum, energy, flags, own, sends, partial, fluid, to_right, to_left, flux):
+def first_kernel(density, momentum, energy, flags, partial, fluid, to_right, to_left, flux, table):
     planes, transverse = 8, 16
     cells = planes * transverse
     for j in range(transverse):
@@ -186,26 +186,28 @@
             at = pl.ds(f * cells + j * planes, planes)
             partial[at, :] = held
             flux[at, :] = moved
+    own, sends = table(0), table(1)
     lines = flux[...]
     sent = lax.dot_general(
-        sends[0], lines, (((1,), (1,)), ((), ())), precision=exact, preferred_element_type=jnp.float32
+        sends[...], lines, (((1,), (1,)), ((), ())), precision=exact, preferred_element_type=jnp.float32
     )
     to_right[...] = sent[0:2]
     to_left[...] = sent[2:4]
     partial[...] = partial[...] + jnp.dot(
-        lines, own[0], precision=exact, preferred_element_type=jnp.float32
-    )
-
-
-def second_kernel(place, partial, fluid, before, after, applied, ends, advanced, summed, upper, lower):
+        lines, own[...], precision=exact, preferred_element_type=jnp.float32
+    )
+
+
+def second_kernel(partial, fluid, before, after, advanced, summed, upper, lower, table):
     planes, transverse = 8, 16
     cells = planes * transverse
     count = partial.shape[0]
+    applied, ends = table(0), table(1)
     received = jnp.concatenate(
         [before[...], after[...], jnp.zeros((4, count), jnp.float32)], axis=0
     )
     added = lax.dot_general(
-        received, applied[0], (((0,), (0,)), ((), ())), precision=exact, preferred_element_type=jnp.float32
+        received, applied[...], (((0,), (0,)), ((), ())), precision=exact, preferred_element_type=jnp.float32
     )
     state = partial[...] + added
     mask = fluid[...]
@@ -217,7 +219,7 @@
         low, high = None, None
         for j in range(transverse):
             row = part[j * planes : (j + 1) * planes]
-            one, two = ends[0, 0, j] * row, ends[0, 0, transverse + j] * row
+            one, two = ends[0, j] * row, ends[0, transverse + j] * row
             low = one if low is None else low + one
             high = two if high is None else high + two
         summed[f * planes : (f + 1) * planes, :] = low
@@ -227,16 +229,17 @@
         lower[f * width : (f + 1) * width, :] = part[:width]
 
 
-def third_kernel(place, gathered, within, prefix, slab):
+def third_kernel(gathered, prefix, slab, table):
     lines = gathered.shape[1] // 2
     outer = slab.shape[0]
-    group = place[1]
+    group = lax.axis_index("gy") // inner
+    within = table(0)
     sums = []
     for kind in range(4):
         side = kind % 2
         total = None
         for k in range(inner):
-            term = within[0, 0, kind * inner + k] * gathered[k, side * lines : (side + 1) * lines, :]
+            term = within[0, kind * inner + k] * gathered[k, side * lines : (side + 1) * lines, :]
             total = term if total is None else total + term
         sums.append(total)
     prefix[:lines, :] = sums[0]
@@ -245,17 +248,18 @@
         slab[other, :, :] = jnp.where(other > group, sums[2], sums[3])
 
 
-def last_kernel(place, advanced, fluid, before, after, prefix, exchanged, table, result):
+def last_kernel(advanced, fluid, before, after, prefix, exchanged, result, table):
     planes, transverse = 8, 16
     cells = planes * transverse
     lines = 5 * planes
     outer = exchanged.shape[0]
     span = transverse + 2 * reach
     base = transverse * span
+    weights = table(0)
     low, high = prefix[:lines, :], prefix[lines:, :]
     for other in range(outer):
-        low = low + table[0, 0, base + 2 * transverse + other] * exchanged[other]
-        high = high + table[0, 0, base + 2 * transverse + outer + other] * exchanged[other]
+        low = low + weights[0, base + 2 * transverse + other] * exchanged[other]
+        high = high + weights[0, base + 2 * transverse + outer + other] * exchanged[other]
     width = reach * planes
 
     def cell(f, k):
@@ -268,7 +272,7 @@
         return after[f * width + k * planes : f * width + (k + 1) * planes, :]
 
     for i in range(transverse):
-        falls, rises = table[0, 0, base + i], table[0, 0, base + transverse + i]
+        falls, rises = weights[0, base + i], weights[0, base + transverse + i]
         sums = [
             falls * low[f * planes : (f + 1) * planes] + rises * high[f * planes : (f + 1) * planes]
             for f in range(5)
@@ -276,7 +280,7 @@
         for k in range(span):
             if k < reach and i >= reach or k >= reach + transverse and i < transverse - reach:
                 continue
-            weight = table[0, 0, i * span + k]
+            weight = weights[0, i * span + k]
             sums = [total + weight * cell(f, k) for f, total in enumerate(sums)]
         keep = fluid[i * planes : (i + 1) * planes, :]
         for f in range(5):
@@ -286,34 +290,44 @@
             result[pl.ds(f * cells + i, planes, stride=transverse), :] = value
 
 
-def whole_block(shape):
-    return pl.BlockSpec(shape, lambda i, place: (0,) * len(shape))
-
-
-def picked_block(table, which, space=None):
-    zeros = (0,) * (table.ndim - 1)
-    shape = (1,) + table.shape[1:]
-    if space is None:
-        return pl.BlockSpec(shape, lambda i, place: (place[which],) + zeros)
-    return pl.BlockSpec(shape, lambda i, place: (place[which],) + zeros, memory_space=space)
-
-
-def call(kernel, name, place, arrays, tables, outs, scratch=()):
-    in_specs = [whole_block(a.shape) for a in arrays]
-    in_specs += [picked_block(table, which, space) for table, which, space in tables]
-    shapes = [jax.ShapeDtypeStruct(shape, jnp.float32) for shape in outs]
+def call(kernel, name, arrays, tables, outs, scratch=(), inside=True, kept=True):
+    given, held, made = len(arrays), len(tables), len(outs)
+
+    def run(*refs):
+        stored = refs[given : given + held]
+        rest = refs[given + held : given + held + made]
+        extra = refs[given + held + made : -held - 1]
+        rows, sems = refs[-held - 1 : -1], refs[-1]
+        copies = [
+            pltpu.make_async_copy(stored[n].at[lax.axis_index(axis)], rows[n], sems.at[n])
+            for n, (_, axis, _) in enumerate(tables)
+        ]
+        for copy in copies:
+            copy.start()
+
+        def table(n):
+            copies[n].wait()
+            return rows[n]
+
+        kernel(*refs[:given], *rest, *extra, table)
+
     return pl.pallas_call(
-        kernel,
-        grid_spec=pltpu.PrefetchScalarGridSpec(
-            num_scalar_prefetch=1,
-            grid=(1,),
-            in_specs=in_specs,
-            out_specs=[whole_block(shape) for shape in outs],
-            scratch_shapes=list(scratch),
-        ),
-        out_shape=shapes,
+        run,
+        in_specs=[pl.BlockSpec(memory_space=pltpu.VMEM)] * given
+        + [pl.BlockSpec(memory_space=pl.ANY)] * held,
+        out_specs=[pl.BlockSpec(memory_space=pltpu.VMEM)] * made,
+        out_shape=[
+            pltpu.VMEM(shape, jnp.float32) if kept else jax.ShapeDtypeStruct(shape, jnp.float32)
+            for shape in outs
+        ],
+        scratch_shapes=list(scratch)
+        + [space(table.shape[1:], jnp.float32) for table, _, space in tables]
+        + [pltpu.SemaphoreType.DMA((held,))],
         name=name,
-    )(place, *arrays, *[jnp.asarray(table) for table, _, _ in tables])
+    )(
+        *[pltpu.with_memory_space_constraint(a, pltpu.VMEM) if inside else a for a in arrays],
+        *[jnp.asarray(table) for table, _, _ in tables],
+    )
 
 
 def body(tables, density, momentum, energy, solid_flags):
@@ -322,34 +336,28 @@
     cells = planes * transverse
     parts, columns = lax.axis_size("gy"), lax.axis_size("gx")
     outer = parts // inner
-    gx, gy = lax.axis_index("gx"), lax.axis_index("gy")
-    place = jnp.stack([gy, gy // inner, gx]).astype(jnp.int32)
-    smem = pltpu.SMEM
+    lines = 5 * planes
     partial, fluid, to_right, to_left = call(
         first_kernel,
         "flux_step",
-        place,
         [
             density.reshape(cells, width),
             momentum.reshape(3 * cells, width),
             energy.reshape(cells, width),
             solid_flags.reshape(cells, width),
         ],
-        [(own, 2, None), (sends, 2, None)],
+        [(own, "gx", pltpu.VMEM), (sends, "gx", pltpu.VMEM)],
         [(5 * cells, width), (cells, width), (2, 5 * cells), (2, 5 * cells)],
         [pltpu.VMEM((5 * cells, width), jnp.float32)],
-    )
-    up = [(i, i + 1) for i in range(columns - 1)]
-    down = [(i + 1, i) for i in range(columns - 1)]
-    before = lax.ppermute(to_right, "gx", up)
-    after = lax.ppermute(to_left, "gx", down)
-    lines = 5 * planes
+        inside=False,
+    )
+    before = lax.ppermute(to_right, "gx", [(i, i + 1) for i in range(columns - 1)])
+    after = lax.ppermute(to_left, "gx", [(i + 1, i) for i in range(columns - 1)])
     advanced, summed, upper, lower = call(
         second_kernel,
         "advance_step",
-        place,
         [partial, fluid, before, after],
-        [(applied, 2, None), (ends, 0, smem)],
+        [(applied, "gx", pltpu.VMEM), (ends, "gy", pltpu.SMEM)],
         [
             (5 * cells, width),
             (2 * lines, width),
@@ -361,29 +369,22 @@
     high_rows = lax.ppermute(lower, "gy", [(i + 1, i) for i in range(parts - 1)])
     near = [[g * inner + k for k in range(inner)] for g in range(outer)]
     far = [[g * inner + k for g in range(outer)] for k in range(inner)]
-    gathered = lax.all_to_all(
-        jnp.broadcast_to(summed[None], (inner, 2 * lines, width)),
-        "gy",
-        0,
-        0,
-        axis_index_groups=near,
-    )
+    gathered = lax.all_gather(summed, "gy", axis_index_groups=near)
     prefix, slab = call(
         third_kernel,
         "group_step",
-        place,
         [gathered],
-        [(within, 0, smem)],
+        [(within, "gy", pltpu.SMEM)],
         [(2 * lines, width), (outer, lines, width)],
     )
     exchanged = lax.all_to_all(slab, "gy", 0, 0, axis_index_groups=far)
     (result,) = call(
         last_kernel,
         "filter_step",
-        place,
         [advanced, fluid, low_rows, high_rows, prefix, exchanged],
-        [(last, 0, smem)],
+        [(last, "gy", pltpu.SMEM)],
         [(5 * cells, width)],
+        kept=False,
     )
     return result.reshape(5, planes, transverse, width)
 

time: 81.1 us -> 68.7 us (0.85)
  the two profiles are of different devices: /device:TPU:36 before, /device:TPU:34 now
where the time goes in v2:
time: 68.7 us; the launch traced here: 68.3 us
  blocking collectives  35.4 us (52%)
  starting transfers between devices  21.9 us (32%)
  Pallas kernels  7.28 us (11%)
  waiting for transfers between devices  3.54 us (5%)
    all_gather x1, blocking collectives, body(): gathered = lax.all_gather(summed, 'gy', axis_index_groups=near)  35.4 us
    pallas_call x4, Pallas kernels, call(): pl.pallas_call(run, in_specs=[pl.BlockSpec(memory_space=pltpu.VMEM)] * gi...  7.28 us
    ppermute x1, starting transfers between devices, body(): lax.ppermute(lower, 'gy', [(i + 1, i) for i in range(parts - 1)])  7.24 us
    all_to_all x1, starting transfers between devices, body(): exchanged = lax.all_to_all(slab, 'gy', 0, 0, axis_index_groups=far)  7.22 us
    ppermute x1, starting transfers between devices, body(): lax.ppermute(to_left, 'gx', [(i + 1, i) for i in range(columns - 1)])  3.64 us
    ppermute x1, starting transfers between devices, body(): lax.ppermute(to_right, 'gx', [(i, i + 1) for i in range(columns - 1)])  1.92 us
    ppermute x1, starting transfers between devices, body(): low_rows = lax.ppermute(upper, 'gy', [(i, i + 1) for i in range(parts - 1)])  1.91 us
    ppermute x1, waiting for transfers between devices, body(): lax.ppermute(lower, 'gy', [(i + 1, i) for i in range(parts - 1)])  1.53 us
  transfers between devices with their start and end apart: 5, of which 3 were waited for; matrix products, arithmetic and copies ran while one was open for 0% of the time, Pallas kernels for 0%

profile of v2, /device:TPU:34, one launch (start us, length us, event | category | flops | bytes accessed | tf_op | source)
XLA Modules:
  0.0 68.3 jit_solution(1424869796178541660)
XLA Ops:
  0.0 2.6 %flux_step.1 = (f32[640,128]{1,0:T(8,128)S(1)}, f32[128,128]{1,0:T(8,128)S(1)}, f32[2,640]{1,0:T(2,128)S(1)}, f32[2,640]{1,0:T(2,128)S(1)}) custom-call(f32[128,128]{1,0:T(8,128)} %bitcast.8, f32[384,128]{1,0:T(8,128)} %bitcast.7, f32[128,128]{1,0:T(8,128)} %bitcast.9, s32[128,128]{1,0:T(8,128)} %bitcast.10, f32[8,128,128]{2,1,0:T(8,128)} %constant.12.clone.refs_4_, ...), custom_call_target="tpu_custom_call" | custom-call | tf_op jit(solution)/shard_map/flux_step/pallas_call | solution.py:314
  2.6 1.9 %collective-permute-start = (f32[2,640]{1,0:T(2,128)S(1)}, f32[2,640]{1,0:T(2,128)S(1)}, u32[]{:S(2)}, u32[]{:S(2)}) collective-permute-start(f32[2,640]{1,0:T(2,128)S(1)} %get-tuple-element.17), channel_id=1, source_target_pairs={{0,96},{96,192},{192,288},{288,384},{384,480},{480,576},{576,672},... | collective-permute-start | bytes 15368 | tf_op jit(solution)/shard_map/ppermute | solution.py:354
  4.5 3.6 %collective-permute-start.1 = (f32[2,640]{1,0:T(2,128)S(1)}, f32[2,640]{1,0:T(2,128)S(1)}, u32[]{:S(2)}, u32[]{:S(2)}) collective-permute-start(f32[2,640]{1,0:T(2,128)S(1)} %get-tuple-element.18), channel_id=1, source_target_pairs={{96,0},{192,96},{288,192},{384,288},{480,384},{576,480},{672,576},... | collective-permute-start | bytes 15368 | tf_op jit(solution)/shard_map/ppermute | solution.py:355
  8.2 0.0 collective-permute-done.refs_2_
  8.2 1.3 %collective-permute-done.1.refs_3_ = f32[2,640]{1,0:T(2,128)S(1)} collective-permute-done((f32[2,640]{1,0:T(2,128)S(1)}, f32[2,640]{1,0:T(2,128)S(1)}, u32[]{:S(2)}, u32[]{:S(2)}) %collective-permute-start.1) | collective-permute-done | bytes 5152 | tf_op jit(solution)/shard_map/ppermute | solution.py:355
  9.5 1.3 %advance_step.1 = (f32[640,128]{1,0:T(8,128)S(1)}, f32[80,128]{1,0:T(8,128)S(1)}, f32[200,128]{1,0:T(8,128)S(1)}, f32[200,128]{1,0:T(8,128)S(1)}) custom-call(f32[640,128]{1,0:T(8,128)S(1)} %get-tuple-element.15.refs_0_, f32[128,128]{1,0:T(8,128)S(1)} %get-tuple-element.16.refs_1_, f32[2,640]{1,0:T(2,128)S(1)} %collective-permute-done.refs_2_, ...), custom_call_target="tpu_custom_call" | custom-call | tf_op jit(solution)/shard_map/advance_step/pallas_call | solution.py:314
  10.8 35.4 %all-gather = f32[960,128]{1,0:T(8,128)S(1)} all-gather(f32[80,128]{1,0:T(8,128)S(1)} %get-tuple-element.22), channel_id=2, replica_groups={{0,1,2,3,4,5,6,7,8,9,10,11},{12,13,14,15,16,17,18,19,20,21,22,23},{24,2..., dimensions={0}, use_global_device_ids=true | all-gather | bytes 532480 | tf_op jit(solution)/shard_map/all_gather | solution.py:372
  46.2 1.4 %group_step.1 = (f32[80,128]{1,0:T(8,128)S(1)}, f32[8,40,128]{2,1,0:T(8,128)}) custom-call(f32[12,80,128]{2,1,0:T(8,128)S(1)} %bitcast.6, f32[96,1,128]{2,1,0:T(1,128)} %constant.16.clone.refs_1_), custom_call_target="tpu_custom_call" | custom-call | tf_op jit(solution)/shard_map/group_step/pallas_call | solution.py:314
  47.6 7.2 %all-to-all-start = ((f32[8,40,128]{2,1,0:T(8,128)}), f32[8,40,128]{2,1,0:T(8,128)S(1)}, u32[]{:S(2)}, u32[]{:S(2)}) async-start(f32[8,40,128]{2,1,0:T(8,128)} %get-tuple-element.24), calls=%async_computation | async-start | bytes 327680 | tf_op jit(solution)/shard_map/all_to_all | solution.py:380
  54.8 1.9 %collective-permute-start.2 = (f32[200,128]{1,0:T(8,128)S(1)}, f32[200,128]{1,0:T(8,128)S(1)}, u32[]{:S(2)}, u32[]{:S(2)}) collective-permute-start(f32[200,128]{1,0:T(8,128)S(1)} %get-tuple-element.20), channel_id=1, source_target_pairs={{0,1},{1,2},{2,3},{3,4},{4,5},{5,6},{6,7},{7,8},{8,9},{9,10},{10,1... | collective-permute-start | bytes 307208 | tf_op jit(solution)/shard_map/ppermute | solution.py:368
  56.7 7.2 %collective-permute-start.3 = (f32[200,128]{1,0:T(8,128)S(1)}, f32[200,128]{1,0:T(8,128)S(1)}, u32[]{:S(2)}, u32[]{:S(2)}) collective-permute-start(f32[200,128]{1,0:T(8,128)S(1)} %get-tuple-element.21), channel_id=1, source_target_pairs={{1,0},{2,1},{3,2},{4,3},{5,4},{6,5},{7,6},{8,7},{9,8},{10,9},{11,1... | collective-permute-start | bytes 307208 | tf_op jit(solution)/shard_map/ppermute | solution.py:369
  64.0 0.7 %collective-permute-done.2.refs_2_ = f32[200,128]{1,0:T(8,128)S(1)} collective-permute-done((f32[200,128]{1,0:T(8,128)S(1)}, f32[200,128]{1,0:T(8,128)S(1)}, u32[]{:S(2)}, u32[]{:S(2)}) %collective-permute-start.2) | collective-permute-done | bytes 102432 | tf_op jit(solution)/shard_map/ppermute | solution.py:368
  64.7 1.5 %collective-permute-done.3.refs_3_ = f32[200,128]{1,0:T(8,128)S(1)} collective-permute-done((f32[200,128]{1,0:T(8,128)S(1)}, f32[200,128]{1,0:T(8,128)S(1)}, u32[]{:S(2)}, u32[]{:S(2)}) %collective-permute-start.3) | collective-permute-done | bytes 102432 | tf_op jit(solution)/shard_map/ppermute | solution.py:369
  66.2 0.0 all-to-all-done.refs_5_
  66.2 2.0 %filter_step.1 = f32[640,128]{1,0:T(8,128)} custom-call(f32[640,128]{1,0:T(8,128)S(1)} %get-tuple-element.19.refs_0_, f32[128,128]{1,0:T(8,128)S(1)} %get-tuple-element.16.refs_1_, f32[200,128]{1,0:T(8,128)S(1)} %collective-permute-done.2.refs_2_, f32[200,128]{1,0:T(8,128)S(1)} %collective-permute-done.3.refs_3_, f32[80,128]{1,0:T(8,128)S(1)} %get-tuple-element.23.refs_4_, ...), custom_call_target="tpu_custom_call" | custom-call | tf_op jit(solution)/shard_map/filter_step/pallas_call | solution.py:314
Async XLA Ops:
  2.6 5.6 %collective-permute-start = (f32[2,640]{1,0:T(2,128)S(1)}, f32[2,640]{1,0:T(2,128)S(1)}, u32[]{:S(2)}, u32[]{:S(2)}) collective-permute-start(f32[2,640]{1,0:T(2,128)S(1)} %get-tuple-element.17), channel_id=1, source_target_pairs={{0,96},{96,192},{192,288},{288,384},{384,480},{480,576},{576,672},... | collective-permute-start | bytes 15368 | tf_op jit(solution)/shard_map/ppermute | solution.py:354
  4.5 5.0 %collective-permute-start.1 = (f32[2,640]{1,0:T(2,128)S(1)}, f32[2,640]{1,0:T(2,128)S(1)}, u32[]{:S(2)}, u32[]{:S(2)}) collective-permute-start(f32[2,640]{1,0:T(2,128)S(1)} %get-tuple-element.18), channel_id=1, source_target_pairs={{96,0},{192,96},{288,192},{384,288},{480,384},{576,480},{672,576},... | collective-permute-start | bytes 15368 | tf_op jit(solution)/shard_map/ppermute | solution.py:355
  47.6 18.6 %all-to-all-start = ((f32[8,40,128]{2,1,0:T(8,128)}), f32[8,40,128]{2,1,0:T(8,128)S(1)}, u32[]{:S(2)}, u32[]{:S(2)}) async-start(f32[8,40,128]{2,1,0:T(8,128)} %get-tuple-element.24), calls=%async_computation | async-start | bytes 327680 | tf_op jit(solution)/shard_map/all_to_all | solution.py:380
  54.8 9.9 %collective-permute-start.2 = (f32[200,128]{1,0:T(8,128)S(1)}, f32[200,128]{1,0:T(8,128)S(1)}, u32[]{:S(2)}, u32[]{:S(2)}) collective-permute-start(f32[200,128]{1,0:T(8,128)S(1)} %get-tuple-element.20), channel_id=1, source_target_pairs={{0,1},{1,2},{2,3},{3,4},{4,5},{5,6},{6,7},{7,8},{8,9},{9,10},{10,1... | collective-permute-start | bytes 307208 | tf_op jit(solution)/shard_map/ppermute | solution.py:368
  56.7 9.5 %collective-permute-start.3 = (f32[200,128]{1,0:T(8,128)S(1)}, f32[200,128]{1,0:T(8,128)S(1)}, u32[]{:S(2)}, u32[]{:S(2)}) collective-permute-start(f32[200,128]{1,0:T(8,128)S(1)} %get-tuple-element.21), channel_id=1, source_target_pairs={{1,0},{2,1},{3,2},{4,3},{5,4},{6,5},{7,6},{8,7},{9,8},{10,9},{11,1... | collective-permute-start | bytes 307208 | tf_op jit(solution)/shard_map/ppermute | solution.py:369

commit v3 on v2

--- a/solution.py
+++ b/solution.py
@@ -1,4 +1,3 @@
-import functools
 import math
 
 import jax
@@ -14,7 +13,7 @@
 filter_alpha = 0.4999
 reach = 5
 inner = 12
-exact = lax.Precision.HIGHEST
+half = jnp.bfloat16
 
 
 def derivative_matrix(length):
@@ -35,27 +34,37 @@
     return np.linalg.solve(left, right)
 
 
+def halves(table):
+    high = table.astype(np.float32).astype(half)
+    low = (table - high.astype(np.float64)).astype(np.float32).astype(half)
+    return high, low
+
+
 def streamwise_tables(parts, width):
     whole = derivative_matrix(parts * width)
     rows = [slice(p * width, (p + 1) * width) for p in range(parts)]
     own = np.stack([whole[rows[p], rows[p]].T for p in range(parts)])
     sends = np.zeros((parts, 8, width))
-    applied = np.zeros((parts, 8, width))
+    applied = np.zeros((parts, 4, width))
     for p in range(parts):
+        above, below = (0, 2) if p % 2 == 0 else (2, 0)
         if p + 1 < parts:
             block = whole[rows[p + 1], rows[p]]
-            sends[p, 0:2] = block[0:2]
-            applied[p + 1, 0, 0] = 1.0
-            applied[p + 1, 1, 1:] = block[1:, -1] / block[1, -1]
+            sends[p, above : above + 2] = block[0:2]
+            block = whole[rows[p], rows[p + 1]]
+            applied[p, above, -1] = 1.0
+            applied[p, above + 1, :-1] = block[:-1, 0] / block[-2, 0]
         if p > 0:
             block = whole[rows[p - 1], rows[p]]
-            sends[p, 2], sends[p, 3] = block[-1], block[-2]
-            applied[p - 1, 2, -1] = 1.0
-            applied[p - 1, 3, :-1] = block[:-1, 0] / block[-2, 0]
+            sends[p, below], sends[p, below + 1] = block[-1], block[-2]
+            block = whole[rows[p], rows[p - 1]]
+            applied[p, below, 0] = 1.0
+            applied[p, below + 1, 1:] = block[1:, -1] / block[1, -1]
+    high, low = halves(-step_size * applied)
     return (
-        (-step_size * own).astype(np.float32),
-        sends.astype(np.float32),
-        (-step_size * applied).astype(np.float32),
+        np.concatenate(halves(-step_size * own), axis=1),
+        np.concatenate(halves(sends), axis=1),
+        np.concatenate([high, high, low, np.zeros_like(low)], axis=1),
     )
 
 
@@ -159,7 +168,9 @@
     return wide
 
 
-def first_kernel(density, momentum, energy, flags, partial, fluid, to_right, to_left, flux, table):
+def first_kernel(
+    density, momentum, energy, flags, partial, fluid, to_first, to_second, flux, table
+):
     planes, transverse = 8, 16
     cells = planes * transverse
     for j in range(transverse):
@@ -186,28 +197,40 @@
             at = pl.ds(f * cells + j * planes, planes)
             partial[at, :] = held
             flux[at, :] = moved
-    own, sends = table(0), table(1)
     lines = flux[...]
-    sent = lax.dot_general(
-        sends[...], lines, (((1,), (1,)), ((), ())), precision=exact, preferred_element_type=jnp.float32
-    )
-    to_right[...] = sent[0:2]
-    to_left[...] = sent[2:4]
-    partial[...] = partial[...] + jnp.dot(
-        lines, own[...], precision=exact, preferred_element_type=jnp.float32
-    )
-
-
-def second_kernel(partial, fluid, before, after, advanced, summed, upper, lower, table):
+    high = lines.astype(half)
+    low = (lines - high.astype(jnp.float32)).astype(half)
+    sends = table(1)[...]
+    main, rest = (
+        lax.dot_general(sends, part, (((1,), (1,)), ((), ())), preferred_element_type=jnp.float32)
+        for part in (high, low)
+    )
+    sent = main[:8] + main[8:] + rest[:8]
+    to_first[...] = sent[0:2]
+    to_second[...] = sent[2:4]
+    own = table(0)
+    width = own.shape[1]
+    coarse, fine = own[:width, :], own[width:, :]
+    partial[...] = partial[...] + (
+        jnp.dot(high, coarse, preferred_element_type=jnp.float32)
+        + jnp.dot(high, fine, preferred_element_type=jnp.float32)
+        + jnp.dot(low, coarse, preferred_element_type=jnp.float32)
+    )
+
+
+def second_kernel(partial, fluid, first, second, advanced, summed, first_rows, second_rows, table):
     planes, transverse = 8, 16
     cells = planes * transverse
-    count = partial.shape[0]
     applied, ends = table(0), table(1)
-    received = jnp.concatenate(
-        [before[...], after[...], jnp.zeros((4, count), jnp.float32)], axis=0
-    )
+    odd = lax.axis_index("gy") % 2 == 1
+    received = jnp.concatenate([first[...], second[...]], axis=0)
+    high = received.astype(half).astype(jnp.float32)
+    stacked = jnp.concatenate([high, received - high, high, jnp.zeros_like(high)], axis=0)
     added = lax.dot_general(
-        received, applied[...], (((0,), (0,)), ((), ())), precision=exact, preferred_element_type=jnp.float32
+        stacked.astype(half),
+        applied[...],
+        (((0,), (0,)), ((), ())),
+        preferred_element_type=jnp.float32,
     )
     state = partial[...] + added
     mask = fluid[...]
@@ -225,8 +248,9 @@
         summed[f * planes : (f + 1) * planes, :] = low
         summed[(5 + f) * planes : (6 + f) * planes, :] = high
         width = reach * planes
-        upper[f * width : (f + 1) * width, :] = part[cells - width :]
-        lower[f * width : (f + 1) * width, :] = part[:width]
+        at = slice(f * width, (f + 1) * width)
+        first_rows[at, :] = jnp.where(odd, part[:width], part[cells - width :])
+        second_rows[at, :] = jnp.where(odd, part[cells - width :], part[:width])
 
 
 def third_kernel(gathered, prefix, slab, table):
@@ -248,7 +272,7 @@
         slab[other, :, :] = jnp.where(other > group, sums[2], sums[3])
 
 
-def last_kernel(advanced, fluid, before, after, prefix, exchanged, result, table):
+def last_kernel(advanced, fluid, first, second, prefix, exchanged, result, table):
     planes, transverse = 8, 16
     cells = planes * transverse
     lines = 5 * planes
@@ -261,15 +285,22 @@
         low = low + weights[0, base + 2 * transverse + other] * exchanged[other]
         high = high + weights[0, base + 2 * transverse + outer + other] * exchanged[other]
     width = reach * planes
+    odd = lax.axis_index("gy") % 2 == 1
+
+    def chosen(one, two, f, k):
+        at = slice(f * width + k * planes, f * width + (k + 1) * planes)
+        return jnp.where(odd, one[at, :], two[at, :])
+
+    before = [[chosen(first, second, f, k) for k in range(reach)] for f in range(5)]
+    after = [[chosen(second, first, f, k) for k in range(reach)] for f in range(5)]
 
     def cell(f, k):
         if k < reach:
-            return before[f * width + k * planes : f * width + (k + 1) * planes, :]
+            return before[f][k]
         k -= reach
         if k < transverse:
             return advanced[f * cells + k * planes : f * cells + (k + 1) * planes, :]
-        k -= transverse
-        return after[f * width + k * planes : f * width + (k + 1) * planes, :]
+        return after[f][k - transverse]
 
     for i in range(transverse):
         falls, rises = weights[0, base + i], weights[0, base + transverse + i]
@@ -290,7 +321,7 @@
             result[pl.ds(f * cells + i, planes, stride=transverse), :] = value
 
 
-def call(kernel, name, arrays, tables, outs, scratch=(), inside=True, kept=True):
+def call(kernel, arrays, tables, outs, scratch=(), inside=True, kept=True):
     given, held, made = len(arrays), len(tables), len(outs)
 
     def run(*refs):
@@ -321,13 +352,19 @@
             for shape in outs
         ],
         scratch_shapes=list(scratch)
-        + [space(table.shape[1:], jnp.float32) for table, _, space in tables]
+        + [space(table.shape[1:], table.dtype) for table, _, space in tables]
         + [pltpu.SemaphoreType.DMA((held,))],
-        name=name,
     )(
         *[pltpu.with_memory_space_constraint(a, pltpu.VMEM) if inside else a for a in arrays],
         *[jnp.asarray(table) for table, _, _ in tables],
     )
+
+
+def pairs(start, count):
+    swaps = []
+    for i in range(start, count - 1, 2):
+        swaps += [(i, i + 1), (i + 1, i)]
+    return swaps
 
 
 def body(tables, density, momentum, energy, solid_flags):
@@ -337,9 +374,8 @@
     parts, columns = lax.axis_size("gy"), lax.axis_size("gx")
     outer = parts // inner
     lines = 5 * planes
-    partial, fluid, to_right, to_left = call(
+    partial, fluid, to_first, to_second = call(
         first_kernel,
-        "flux_step",
         [
             density.reshape(cells, width),
             momentum.reshape(3 * cells, width),
@@ -351,12 +387,11 @@
         [pltpu.VMEM((5 * cells, width), jnp.float32)],
         inside=False,
     )
-    before = lax.ppermute(to_right, "gx", [(i, i + 1) for i in range(columns - 1)])
-    after = lax.ppermute(to_left, "gx", [(i + 1, i) for i in range(columns - 1)])
-    advanced, summed, upper, lower = call(
+    second = lax.ppermute(to_second, "gx", pairs(1, columns))
+    first = lax.ppermute(to_first, "gx", pairs(0, columns))
+    advanced, summed, first_rows, second_rows = call(
         second_kernel,
-        "advance_step",
-        [partial, fluid, before, after],
+        [partial, fluid, first, second],
         [(applied, "gx", pltpu.VMEM), (ends, "gy", pltpu.SMEM)],
         [
             (5 * cells, width),
@@ -365,14 +400,13 @@
             (reach * lines, width),
         ],
     )
-    low_rows = lax.ppermute(upper, "gy", [(i, i + 1) for i in range(parts - 1)])
-    high_rows = lax.ppermute(lower, "gy", [(i + 1, i) for i in range(parts - 1)])
+    first_rows = lax.ppermute(first_rows, "gy", pairs(0, parts))
+    second_rows = lax.ppermute(second_rows, "gy", pairs(1, parts))
     near = [[g * inner + k for k in range(inner)] for g in range(outer)]
     far = [[g * inner + k for g in range(outer)] for k in range(inner)]
     gathered = lax.all_gather(summed, "gy", axis_index_groups=near)
     prefix, slab = call(
         third_kernel,
-        "group_step",
         [gathered],
         [(within, "gy", pltpu.SMEM)],
         [(2 * lines, width), (outer, lines, width)],
@@ -380,8 +414,7 @@
     exchanged = lax.all_to_all(slab, "gy", 0, 0, axis_index_groups=far)
     (result,) = call(
         last_kernel,
-        "filter_step",
-        [advanced, fluid, low_rows, high_rows, prefix, exchanged],
+        [advanced, fluid, first_rows, second_rows, prefix, exchanged],
         [(last, "gy", pltpu.SMEM)],
         [(5 * cells, width)],
         kept=False,
@@ -400,8 +433,12 @@
         P(None, "gy", "gx"),
         P(None, "gy", "gx"),
     )
+
+    def step(*arrays):
+        return body(tables, *arrays)
+
     return jax.shard_map(
-        functools.partial(body, tables),
+        step,
         mesh=mesh,
         in_specs=placed,
         out_specs=P(None, None, "gy", "gx"),

time: 68.7 us -> 68.4 us (level)
  the two profiles are of different devices: /device:TPU:34 before, /device:TPU:38 now
where the time goes in v3:
time: 68.4 us; the launch traced here: 68 us
  blocking collectives  35.3 us (52%)
  starting transfers between devices  16.6 us (24%)
  waiting for transfers between devices  9.24 us (14%)
  Pallas kernels  6.74 us (10%)
    all_gather x1, blocking collectives, body(): gathered = lax.all_gather(summed, 'gy', axis_index_groups=near)  35.3 us
    all_to_all x1, starting transfers between devices, body(): exchanged = lax.all_to_all(slab, 'gy', 0, 0, axis_index_groups=far)  7.22 us
    pallas_call x4, Pallas kernels, call(): pl.pallas_call(run, in_specs=[pl.BlockSpec(memory_space=pltpu.VMEM)] * gi...  6.74 us
    ppermute x1, waiting for transfers between devices, body(): second_rows = lax.ppermute(second_rows, 'gy', pairs(1, parts))  5.25 us
    ppermute x1, starting transfers between devices, body(): second = lax.ppermute(to_second, 'gx', pairs(1, columns))  2.84 us
    ppermute x1, starting transfers between devices, body(): second_rows = lax.ppermute(second_rows, 'gy', pairs(1, parts))  2.71 us
    ppermute x1, waiting for transfers between devices, body(): second = lax.ppermute(to_second, 'gx', pairs(1, columns))  2.08 us
    ppermute x1, starting transfers between devices, body(): first = lax.ppermute(to_first, 'gx', pairs(0, columns))  1.92 us
  transfers between devices with their start and end apart: 5, of which 3 were waited for; matrix products, arithmetic and copies ran while one was open for 0% of the time, Pallas kernels for 0%

profile of v3, /device:TPU:38, one launch (start us, length us, event | category | flops | bytes accessed | tf_op | source)
XLA Modules:
  0.0 68.0 jit_solution(8318227610936761873)
XLA Ops:
  0.0 2.2 %shard_map.100 = (f32[640,128]{1,0:T(8,128)S(1)}, f32[128,128]{1,0:T(8,128)S(1)}, f32[2,640]{1,0:T(2,128)S(1)}, f32[2,640]{1,0:T(2,128)S(1)}) custom-call(f32[128,128]{1,0:T(8,128)} %bitcast.8, f32[384,128]{1,0:T(8,128)} %bitcast.7, f32[128,128]{1,0:T(8,128)} %bitcast.9, s32[128,128]{1,0:T(8,128)} %bitcast.10, bf16[8,256,128]{2,1,0:T(8,128)(2,1)} %constant.12.clone.refs_4_, ...), custom_call_target="tpu_custom_call" | custom-call | tf_op jit(solution)/shard_map/pallas_call | solution.py:345
  2.2 1.9 %collective-permute-start = (f32[2,640]{1,0:T(2,128)S(1)}, f32[2,640]{1,0:T(2,128)S(1)}, u32[]{:S(2)}, u32[]{:S(2)}) collective-permute-start(f32[2,640]{1,0:T(2,128)S(1)} %get-tuple-element.17), channel_id=1, source_target_pairs={{0,96},{96,0},{192,288},{288,192},{384,480},{480,384},{576,672},{6... | collective-permute-start | bytes 15368 | tf_op jit(solution)/shard_map/ppermute | solution.py:391
  4.2 2.8 %collective-permute-start.1 = (f32[2,640]{1,0:T(2,128)S(1)}, f32[2,640]{1,0:T(2,128)S(1)}, u32[]{:S(2)}, u32[]{:S(2)}) collective-permute-start(f32[2,640]{1,0:T(2,128)S(1)} %get-tuple-element.18), channel_id=1, source_target_pairs={{96,192},{192,96},{288,384},{384,288},{480,576},{576,480},{97,193}... | collective-permute-start | bytes 15368 | tf_op jit(solution)/shard_map/ppermute | solution.py:390
  7.0 0.0 collective-permute-done.refs_2_
  7.0 2.1 %collective-permute-done.1.refs_3_ = f32[2,640]{1,0:T(2,128)S(1)} collective-permute-done((f32[2,640]{1,0:T(2,128)S(1)}, f32[2,640]{1,0:T(2,128)S(1)}, u32[]{:S(2)}, u32[]{:S(2)}) %collective-permute-start.1) | collective-permute-done | bytes 5152 | tf_op jit(solution)/shard_map/ppermute | solution.py:390
  9.1 1.1 %shard_map.101 = (f32[640,128]{1,0:T(8,128)S(1)}, f32[80,128]{1,0:T(8,128)S(1)}, f32[200,128]{1,0:T(8,128)S(1)}, f32[200,128]{1,0:T(8,128)S(1)}) custom-call(f32[640,128]{1,0:T(8,128)S(1)} %get-tuple-element.15.refs_0_, f32[128,128]{1,0:T(8,128)S(1)} %get-tuple-element.16.refs_1_, f32[2,640]{1,0:T(2,128)S(1)} %collective-permute-done.refs_2_, ...), custom_call_target="tpu_custom_call" | custom-call | tf_op jit(solution)/shard_map/pallas_call | solution.py:345
  10.2 35.3 %all-gather = f32[960,128]{1,0:T(8,128)S(1)} all-gather(f32[80,128]{1,0:T(8,128)S(1)} %get-tuple-element.22), channel_id=2, replica_groups={{0,1,2,3,4,5,6,7,8,9,10,11},{12,13,14,15,16,17,18,19,20,21,22,23},{24,2..., dimensions={0}, use_global_device_ids=true | all-gather | bytes 532480 | tf_op jit(solution)/shard_map/all_gather | solution.py:407
  45.5 1.4 %shard_map.102 = (f32[80,128]{1,0:T(8,128)S(1)}, f32[8,40,128]{2,1,0:T(8,128)}) custom-call(f32[12,80,128]{2,1,0:T(8,128)S(1)} %bitcast.6, f32[96,1,128]{2,1,0:T(1,128)} %constant.16.clone.refs_1_), custom_call_target="tpu_custom_call" | custom-call | tf_op jit(solution)/shard_map/pallas_call | solution.py:345
  46.9 7.2 %all-to-all-start = ((f32[8,40,128]{2,1,0:T(8,128)}), f32[8,40,128]{2,1,0:T(8,128)S(1)}, u32[]{:S(2)}, u32[]{:S(2)}) async-start(f32[8,40,128]{2,1,0:T(8,128)} %get-tuple-element.24), calls=%async_computation | async-start | bytes 327680 | tf_op jit(solution)/shard_map/all_to_all | solution.py:414
  54.1 1.9 %collective-permute-start.2 = (f32[200,128]{1,0:T(8,128)S(1)}, f32[200,128]{1,0:T(8,128)S(1)}, u32[]{:S(2)}, u32[]{:S(2)}) collective-permute-start(f32[200,128]{1,0:T(8,128)S(1)} %get-tuple-element.20), channel_id=1, source_target_pairs={{0,1},{1,0},{2,3},{3,2},{4,5},{5,4},{6,7},{7,6},{8,9},{9,8},{10,11... | collective-permute-start | bytes 307208 | tf_op jit(solution)/shard_map/ppermute | solution.py:403
  56.0 2.7 %collective-permute-start.3 = (f32[200,128]{1,0:T(8,128)S(1)}, f32[200,128]{1,0:T(8,128)S(1)}, u32[]{:S(2)}, u32[]{:S(2)}) collective-permute-start(f32[200,128]{1,0:T(8,128)S(1)} %get-tuple-element.21), channel_id=1, source_target_pairs={{1,2},{2,1},{3,4},{4,3},{5,6},{6,5},{7,8},{8,7},{9,10},{10,9},{11,... | collective-permute-start | bytes 307208 | tf_op jit(solution)/shard_map/ppermute | solution.py:404
  58.8 1.9 %collective-permute-done.2.refs_2_ = f32[200,128]{1,0:T(8,128)S(1)} collective-permute-done((f32[200,128]{1,0:T(8,128)S(1)}, f32[200,128]{1,0:T(8,128)S(1)}, u32[]{:S(2)}, u32[]{:S(2)}) %collective-permute-start.2) | collective-permute-done | bytes 102432 | tf_op jit(solution)/shard_map/ppermute | solution.py:403
  60.7 5.2 %collective-permute-done.3.refs_3_ = f32[200,128]{1,0:T(8,128)S(1)} collective-permute-done((f32[200,128]{1,0:T(8,128)S(1)}, f32[200,128]{1,0:T(8,128)S(1)}, u32[]{:S(2)}, u32[]{:S(2)}) %collective-permute-start.3) | collective-permute-done | bytes 102432 | tf_op jit(solution)/shard_map/ppermute | solution.py:404
  65.9 0.0 all-to-all-done.refs_5_
  65.9 2.0 %shard_map.103 = f32[640,128]{1,0:T(8,128)} custom-call(f32[640,128]{1,0:T(8,128)S(1)} %get-tuple-element.19.refs_0_, f32[128,128]{1,0:T(8,128)S(1)} %get-tuple-element.16.refs_1_, f32[200,128]{1,0:T(8,128)S(1)} %collective-permute-done.2.refs_2_, f32[200,128]{1,0:T(8,128)S(1)} %collective-permute-done.3.refs_3_, f32[80,128]{1,0:T(8,128)S(1)} %get-tuple-element.23.refs_4_, ...), custom_call_target="tpu_custom_call" | custom-call | tf_op jit(solution)/shard_map/pallas_call | solution.py:345
Async XLA Ops:
  2.2 4.8 %collective-permute-start = (f32[2,640]{1,0:T(2,128)S(1)}, f32[2,640]{1,0:T(2,128)S(1)}, u32[]{:S(2)}, u32[]{:S(2)}) collective-permute-start(f32[2,640]{1,0:T(2,128)S(1)} %get-tuple-element.17), channel_id=1, source_target_pairs={{0,96},{96,0},{192,288},{288,192},{384,480},{480,384},{576,672},{6... | collective-permute-start | bytes 15368 | tf_op jit(solution)/shard_map/ppermute | solution.py:391
  4.2 4.9 %collective-permute-start.1 = (f32[2,640]{1,0:T(2,128)S(1)}, f32[2,640]{1,0:T(2,128)S(1)}, u32[]{:S(2)}, u32[]{:S(2)}) collective-permute-start(f32[2,640]{1,0:T(2,128)S(1)} %get-tuple-element.18), channel_id=1, source_target_pairs={{96,192},{192,96},{288,384},{384,288},{480,576},{576,480},{97,193}... | collective-permute-start | bytes 15368 | tf_op jit(solution)/shard_map/ppermute | solution.py:390
  46.9 19.0 %all-to-all-start = ((f32[8,40,128]{2,1,0:T(8,128)}), f32[8,40,128]{2,1,0:T(8,128)S(1)}, u32[]{:S(2)}, u32[]{:S(2)}) async-start(f32[8,40,128]{2,1,0:T(8,128)} %get-tuple-element.24), calls=%async_computation | async-start | bytes 327680 | tf_op jit(solution)/shard_map/all_to_all | solution.py:414
  54.1 6.5 %collective-permute-start.2 = (f32[200,128]{1,0:T(8,128)S(1)}, f32[200,128]{1,0:T(8,128)S(1)}, u32[]{:S(2)}, u32[]{:S(2)}) collective-permute-start(f32[200,128]{1,0:T(8,128)S(1)} %get-tuple-element.20), channel_id=1, source_target_pairs={{0,1},{1,0},{2,3},{3,2},{4,5},{5,4},{6,7},{7,6},{8,9},{9,8},{10,11... | collective-permute-start | bytes 307208 | tf_op jit(solution)/shard_map/ppermute | solution.py:403
  56.0 9.9 %collective-permute-start.3 = (f32[200,128]{1,0:T(8,128)S(1)}, f32[200,128]{1,0:T(8,128)S(1)}, u32[]{:S(2)}, u32[]{:S(2)}) collective-permute-start(f32[200,128]{1,0:T(8,128)S(1)} %get-tuple-element.21), channel_id=1, source_target_pairs={{1,2},{2,1},{3,4},{4,3},{5,6},{6,5},{7,8},{8,7},{9,10},{10,9},{11,... | collective-permute-start | bytes 307208 | tf_op jit(solution)/shard_map/ppermute | solution.py:404

commit v4 on v3

--- a/solution.py
+++ b/solution.py
@@ -321,42 +321,50 @@
             result[pl.ds(f * cells + i, planes, stride=transverse), :] = value
 
 
-def call(kernel, arrays, tables, outs, scratch=(), inside=True, kept=True):
-    given, held, made = len(arrays), len(tables), len(outs)
+def call(kernel, arrays, tables, outs, scratch=(), rows=(), ahead=(), inside=True, kept=True):
+    given, held, made = len(arrays) + len(rows), len(tables) + len(ahead), len(outs)
 
     def run(*refs):
         stored = refs[given : given + held]
         rest = refs[given + held : given + held + made]
-        extra = refs[given + held + made : -held - 1]
-        rows, sems = refs[-held - 1 : -1], refs[-1]
+        put = refs[given + held + made : given + held + made + len(ahead)]
+        extra = refs[given + held + made + len(ahead) : len(refs) - 1 - len(tables)]
+        extra, sems = (extra, refs[-1]) if held else (refs[given + held + made :], None)
+        placed = (*refs[len(refs) - 1 - len(tables) : -1], *put)
         copies = [
-            pltpu.make_async_copy(stored[n].at[lax.axis_index(axis)], rows[n], sems.at[n])
-            for n, (_, axis, _) in enumerate(tables)
+            pltpu.make_async_copy(stored[n].at[lax.axis_index(axis)], placed[n], sems.at[n])
+            for n, (_, axis) in enumerate([t[:2] for t in tables] + [t[:2] for t in ahead])
         ]
         for copy in copies:
             copy.start()
 
         def table(n):
+            if n >= len(tables):
+                return refs[len(arrays) + n - len(tables)]
             copies[n].wait()
-            return rows[n]
-
-        kernel(*refs[:given], *rest, *extra, table)
-
+            return placed[n]
+
+        kernel(*refs[: len(arrays)], *rest, *extra, table)
+        for copy in copies[len(tables) :]:
+            copy.wait()
+
+    vmem, smem = pl.BlockSpec(memory_space=pltpu.VMEM), pl.BlockSpec(memory_space=pltpu.SMEM)
     return pl.pallas_call(
         run,
-        in_specs=[pl.BlockSpec(memory_space=pltpu.VMEM)] * given
-        + [pl.BlockSpec(memory_space=pl.ANY)] * held,
-        out_specs=[pl.BlockSpec(memory_space=pltpu.VMEM)] * made,
+        in_specs=[vmem] * len(arrays) + [smem] * len(rows) + [pl.BlockSpec(memory_space=pl.ANY)] * held,
+        out_specs=[vmem] * made + [smem] * len(ahead),
         out_shape=[
             pltpu.VMEM(shape, jnp.float32) if kept else jax.ShapeDtypeStruct(shape, jnp.float32)
             for shape in outs
-        ],
+        ]
+        + [pltpu.SMEM(table.shape[1:], jnp.float32) for table, _ in ahead],
         scratch_shapes=list(scratch)
         + [space(table.shape[1:], table.dtype) for table, _, space in tables]
-        + [pltpu.SemaphoreType.DMA((held,))],
+        + ([pltpu.SemaphoreType.DMA((held,))] if held else []),
     )(
         *[pltpu.with_memory_space_constraint(a, pltpu.VMEM) if inside else a for a in arrays],
-        *[jnp.asarray(table) for table, _, _ in tables],
+        *[pltpu.with_memory_space_constraint(row, pltpu.SMEM) for row in rows],
+        *[jnp.asarray(t[0]) for t in (*tables, *ahead)],
     )
 
 
@@ -374,7 +382,7 @@
     parts, columns = lax.axis_size("gy"), lax.axis_size("gx")
     outer = parts // inner
     lines = 5 * planes
-    partial, fluid, to_first, to_second = call(
+    partial, fluid, to_first, to_second, within_row, last_row = call(
         first_kernel,
         [
             density.reshape(cells, width),
@@ -385,6 +393,7 @@
         [(own, "gx", pltpu.VMEM), (sends, "gx", pltpu.VMEM)],
         [(5 * cells, width), (cells, width), (2, 5 * cells), (2, 5 * cells)],
         [pltpu.VMEM((5 * cells, width), jnp.float32)],
+        ahead=[(within, "gy"), (last, "gy")],
         inside=False,
     )
     second = lax.ppermute(to_second, "gx", pairs(1, columns))
@@ -406,17 +415,15 @@
     far = [[g * inner + k for g in range(outer)] for k in range(inner)]
     gathered = lax.all_gather(summed, "gy", axis_index_groups=near)
     prefix, slab = call(
-        third_kernel,
-        [gathered],
-        [(within, "gy", pltpu.SMEM)],
-        [(2 * lines, width), (outer, lines, width)],
+        third_kernel, [gathered], [], [(2 * lines, width), (outer, lines, width)], rows=[within_row]
     )
     exchanged = lax.all_to_all(slab, "gy", 0, 0, axis_index_groups=far)
     (result,) = call(
         last_kernel,
         [advanced, fluid, first_rows, second_rows, prefix, exchanged],
-        [(last, "gy", pltpu.SMEM)],
+        [],
         [(5 * cells, width)],
+        rows=[last_row],
         kept=False,
     )
     return result.reshape(5, planes, transverse, width)

time: 68.4 us -> 67 us (0.980)
  Pallas kernels: 6.74 us -> 5.41 us
    pallas_call x4, Pallas kernels: 6.74 us -> 5.41 us  [call(): pl.pallas_call(run, in_specs=[vmem] * len(arrays) + [smem] * len(rows) +...]
where the time goes in v4:
time: 67 us; the launch traced here: 66.6 us
  blocking collectives  35.3 us (53%)
  starting transfers between devices  16.6 us (25%)
  waiting for transfers between devices  9.24 us (14%)
  Pallas kernels  5.41 us (8%)
    all_gather x1, blocking collectives, body(): gathered = lax.all_gather(summed, 'gy', axis_index_groups=near)  35.3 us
    all_to_all x1, starting transfers between devices, body(): exchanged = lax.all_to_all(slab, 'gy', 0, 0, axis_index_groups=far)  7.21 us
    pallas_call x4, Pallas kernels, call(): pl.pallas_call(run, in_specs=[vmem] * len(arrays) + [smem] * len(rows) +...  5.41 us
    ppermute x1, waiting for transfers between devices, body(): second_rows = lax.ppermute(second_rows, 'gy', pairs(1, parts))  5.25 us
    ppermute x1, starting transfers between devices, body(): second = lax.ppermute(to_second, 'gx', pairs(1, columns))  2.84 us
    ppermute x1, starting transfers between devices, body(): second_rows = lax.ppermute(second_rows, 'gy', pairs(1, parts))  2.71 us
    ppermute x1, waiting for transfers between devices, body(): second = lax.ppermute(to_second, 'gx', pairs(1, columns))  2.08 us
    ppermute x1, starting transfers between devices, body(): first = lax.ppermute(to_first, 'gx', pairs(0, columns))  1.92 us
  transfers between devices with their start and end apart: 5, of which 3 were waited for; matrix products, arithmetic and copies ran while one was open for 0% of the time, Pallas kernels for 0%

profile of v4, /device:TPU:38, one launch (start us, length us, event | category | flops | bytes accessed | tf_op | source)
XLA Modules:
  0.0 66.6 jit_solution(17224020145646652516)
XLA Ops:
  0.0 2.3 %shard_map.100 = (f32[640,128]{1,0:T(8,128)S(1)}, f32[128,128]{1,0:T(8,128)S(1)}, f32[2,640]{1,0:T(2,128)S(1)}, f32[2,640]{1,0:T(2,128)S(1)}, f32[1,128]{1,0:T(1,128)S(4)}, /*index=5*/f32[1,512]{1,0:T(1,128)S(4)}) custom-call(f32[128,128]{1,0:T(8,128)} %bitcast.8, f32[384,128]{1,0:T(8,128)} %bitcast.7, f32[128,128]{1,0:T(8,128)} %bitcast.9, ...), custom_call_target="tpu_custom_call" | custom-call | tf_op jit(solution)/shard_map/pallas_call | solution.py:352
  2.3 1.9 %collective-permute-start = (f32[2,640]{1,0:T(2,128)S(1)}, f32[2,640]{1,0:T(2,128)S(1)}, u32[]{:S(2)}, u32[]{:S(2)}) collective-permute-start(f32[2,640]{1,0:T(2,128)S(1)} %get-tuple-element.19), channel_id=1, source_target_pairs={{0,96},{96,0},{192,288},{288,192},{384,480},{480,384},{576,672},{6... | collective-permute-start | bytes 15368 | tf_op jit(solution)/shard_map/ppermute | solution.py:400
  4.2 2.8 %collective-permute-start.1 = (f32[2,640]{1,0:T(2,128)S(1)}, f32[2,640]{1,0:T(2,128)S(1)}, u32[]{:S(2)}, u32[]{:S(2)}) collective-permute-start(f32[2,640]{1,0:T(2,128)S(1)} %get-tuple-element.20), channel_id=1, source_target_pairs={{96,192},{192,96},{288,384},{384,288},{480,576},{576,480},{97,193}... | collective-permute-start | bytes 15368 | tf_op jit(solution)/shard_map/ppermute | solution.py:399
  7.1 0.0 collective-permute-done.refs_2_
  7.1 2.1 %collective-permute-done.1.refs_3_ = f32[2,640]{1,0:T(2,128)S(1)} collective-permute-done((f32[2,640]{1,0:T(2,128)S(1)}, f32[2,640]{1,0:T(2,128)S(1)}, u32[]{:S(2)}, u32[]{:S(2)}) %collective-permute-start.1) | collective-permute-done | bytes 5152 | tf_op jit(solution)/shard_map/ppermute | solution.py:399
  9.1 1.1 %shard_map.101 = (f32[640,128]{1,0:T(8,128)S(1)}, f32[80,128]{1,0:T(8,128)S(1)}, f32[200,128]{1,0:T(8,128)S(1)}, f32[200,128]{1,0:T(8,128)S(1)}) custom-call(f32[640,128]{1,0:T(8,128)S(1)} %get-tuple-element.17.refs_0_, f32[128,128]{1,0:T(8,128)S(1)} %get-tuple-element.18.refs_1_, f32[2,640]{1,0:T(2,128)S(1)} %collective-permute-done.refs_2_, ...), custom_call_target="tpu_custom_call" | custom-call | tf_op jit(solution)/shard_map/pallas_call | solution.py:352
  10.2 35.3 %all-gather = f32[960,128]{1,0:T(8,128)S(1)} all-gather(f32[80,128]{1,0:T(8,128)S(1)} %get-tuple-element.24), channel_id=2, replica_groups={{0,1,2,3,4,5,6,7,8,9,10,11},{12,13,14,15,16,17,18,19,20,21,22,23},{24,2..., dimensions={0}, use_global_device_ids=true | all-gather | bytes 532480 | tf_op jit(solution)/shard_map/all_gather | solution.py:416
  45.5 0.7 %shard_map.102 = (f32[80,128]{1,0:T(8,128)S(1)}, f32[8,40,128]{2,1,0:T(8,128)}) custom-call(f32[12,80,128]{2,1,0:T(8,128)S(1)} %bitcast.6, f32[1,128]{1,0:T(1,128)S(4)} %get-tuple-element.25.refs_1_), custom_call_target="tpu_custom_call" | custom-call | tf_op jit(solution)/shard_map/pallas_call | solution.py:352
  46.3 7.2 %all-to-all-start = ((f32[8,40,128]{2,1,0:T(8,128)}), f32[8,40,128]{2,1,0:T(8,128)S(1)}, u32[]{:S(2)}, u32[]{:S(2)}) async-start(f32[8,40,128]{2,1,0:T(8,128)} %get-tuple-element.27), calls=%async_computation | async-start | bytes 327680 | tf_op jit(solution)/shard_map/all_to_all | solution.py:420
  53.5 1.9 %collective-permute-start.2 = (f32[200,128]{1,0:T(8,128)S(1)}, f32[200,128]{1,0:T(8,128)S(1)}, u32[]{:S(2)}, u32[]{:S(2)}) collective-permute-start(f32[200,128]{1,0:T(8,128)S(1)} %get-tuple-element.22), channel_id=1, source_target_pairs={{0,1},{1,0},{2,3},{3,2},{4,5},{5,4},{6,7},{7,6},{8,9},{9,8},{10,11... | collective-permute-start | bytes 307208 | tf_op jit(solution)/shard_map/ppermute | solution.py:412
  55.4 2.7 %collective-permute-start.3 = (f32[200,128]{1,0:T(8,128)S(1)}, f32[200,128]{1,0:T(8,128)S(1)}, u32[]{:S(2)}, u32[]{:S(2)}) collective-permute-start(f32[200,128]{1,0:T(8,128)S(1)} %get-tuple-element.23), channel_id=1, source_target_pairs={{1,2},{2,1},{3,4},{4,3},{5,6},{6,5},{7,8},{8,7},{9,10},{10,9},{11,... | collective-permute-start | bytes 307208 | tf_op jit(solution)/shard_map/ppermute | solution.py:413
  58.1 1.9 %collective-permute-done.2.refs_2_ = f32[200,128]{1,0:T(8,128)S(1)} collective-permute-done((f32[200,128]{1,0:T(8,128)S(1)}, f32[200,128]{1,0:T(8,128)S(1)}, u32[]{:S(2)}, u32[]{:S(2)}) %collective-permute-start.2) | collective-permute-done | bytes 102432 | tf_op jit(solution)/shard_map/ppermute | solution.py:412
  60.0 5.2 %collective-permute-done.3.refs_3_ = f32[200,128]{1,0:T(8,128)S(1)} collective-permute-done((f32[200,128]{1,0:T(8,128)S(1)}, f32[200,128]{1,0:T(8,128)S(1)}, u32[]{:S(2)}, u32[]{:S(2)}) %collective-permute-start.3) | collective-permute-done | bytes 102432 | tf_op jit(solution)/shard_map/ppermute | solution.py:413
  65.3 0.0 all-to-all-done.refs_5_
  65.3 1.3 %shard_map.103 = f32[640,128]{1,0:T(8,128)} custom-call(f32[640,128]{1,0:T(8,128)S(1)} %get-tuple-element.21.refs_0_, f32[128,128]{1,0:T(8,128)S(1)} %get-tuple-element.18.refs_1_, f32[200,128]{1,0:T(8,128)S(1)} %collective-permute-done.2.refs_2_, f32[200,128]{1,0:T(8,128)S(1)} %collective-permute-done.3.refs_3_, f32[80,128]{1,0:T(8,128)S(1)} %get-tuple-element.26.refs_4_, ...), custom_call_target="tpu_custom_call" | custom-call | tf_op jit(solution)/shard_map/pallas_call | solution.py:352
Async XLA Ops:
  2.3 4.8 %collective-permute-start = (f32[2,640]{1,0:T(2,128)S(1)}, f32[2,640]{1,0:T(2,128)S(1)}, u32[]{:S(2)}, u32[]{:S(2)}) collective-permute-start(f32[2,640]{1,0:T(2,128)S(1)} %get-tuple-element.19), channel_id=1, source_target_pairs={{0,96},{96,0},{192,288},{288,192},{384,480},{480,384},{576,672},{6... | collective-permute-start | bytes 15368 | tf_op jit(solution)/shard_map/ppermute | solution.py:400
  4.2 4.9 %collective-permute-start.1 = (f32[2,640]{1,0:T(2,128)S(1)}, f32[2,640]{1,0:T(2,128)S(1)}, u32[]{:S(2)}, u32[]{:S(2)}) collective-permute-start(f32[2,640]{1,0:T(2,128)S(1)} %get-tuple-element.20), channel_id=1, source_target_pairs={{96,192},{192,96},{288,384},{384,288},{480,576},{576,480},{97,193}... | collective-permute-start | bytes 15368 | tf_op jit(solution)/shard_map/ppermute | solution.py:399
  46.3 19.0 %all-to-all-start = ((f32[8,40,128]{2,1,0:T(8,128)}), f32[8,40,128]{2,1,0:T(8,128)S(1)}, u32[]{:S(2)}, u32[]{:S(2)}) async-start(f32[8,40,128]{2,1,0:T(8,128)} %get-tuple-element.27), calls=%async_computation | async-start | bytes 327680 | tf_op jit(solution)/shard_map/all_to_all | solution.py:420
  53.5 6.5 %collective-permute-start.2 = (f32[200,128]{1,0:T(8,128)S(1)}, f32[200,128]{1,0:T(8,128)S(1)}, u32[]{:S(2)}, u32[]{:S(2)}) collective-permute-start(f32[200,128]{1,0:T(8,128)S(1)} %get-tuple-element.22), channel_id=1, source_target_pairs={{0,1},{1,0},{2,3},{3,2},{4,5},{5,4},{6,7},{7,6},{8,9},{9,8},{10,11... | collective-permute-start | bytes 307208 | tf_op jit(solution)/shard_map/ppermute | solution.py:412
  55.4 9.9 %collective-permute-start.3 = (f32[200,128]{1,0:T(8,128)S(1)}, f32[200,128]{1,0:T(8,128)S(1)}, u32[]{:S(2)}, u32[]{:S(2)}) collective-permute-start(f32[200,128]{1,0:T(8,128)S(1)} %get-tuple-element.23), channel_id=1, source_target_pairs={{1,2},{2,1},{3,4},{4,3},{5,6},{6,5},{7,8},{8,7},{9,10},{10,9},{11,... | collective-permute-start | bytes 307208 | tf_op jit(solution)/shard_map/ppermute | solution.py:413

commit v5 on v4

--- a/solution.py
+++ b/solution.py
@@ -348,22 +348,24 @@
         for copy in copies[len(tables) :]:
             copy.wait()
 
-    vmem, smem = pl.BlockSpec(memory_space=pltpu.VMEM), pl.BlockSpec(memory_space=pltpu.SMEM)
+    vmem = pl.BlockSpec(memory_space=pltpu.VMEM)
     return pl.pallas_call(
         run,
-        in_specs=[vmem] * len(arrays) + [smem] * len(rows) + [pl.BlockSpec(memory_space=pl.ANY)] * held,
-        out_specs=[vmem] * made + [smem] * len(ahead),
+        in_specs=[vmem] * len(arrays)
+        + [pl.BlockSpec(memory_space=space) for _, space in rows]
+        + [pl.BlockSpec(memory_space=pl.ANY)] * held,
+        out_specs=[vmem] * made + [pl.BlockSpec(memory_space=space) for _, _, space in ahead],
         out_shape=[
             pltpu.VMEM(shape, jnp.float32) if kept else jax.ShapeDtypeStruct(shape, jnp.float32)
             for shape in outs
         ]
-        + [pltpu.SMEM(table.shape[1:], jnp.float32) for table, _ in ahead],
+        + [space(table.shape[1:], table.dtype) for table, _, space in ahead],
         scratch_shapes=list(scratch)
         + [space(table.shape[1:], table.dtype) for table, _, space in tables]
         + ([pltpu.SemaphoreType.DMA((held,))] if held else []),
     )(
         *[pltpu.with_memory_space_constraint(a, pltpu.VMEM) if inside else a for a in arrays],
-        *[pltpu.with_memory_space_constraint(row, pltpu.SMEM) for row in rows],
+        *[pltpu.with_memory_space_constraint(row, space) for row, space in rows],
         *[jnp.asarray(t[0]) for t in (*tables, *ahead)],
     )
 
@@ -382,7 +384,7 @@
     parts, columns = lax.axis_size("gy"), lax.axis_size("gx")
     outer = parts // inner
     lines = 5 * planes
-    partial, fluid, to_first, to_second, within_row, last_row = call(
+    partial, fluid, to_first, to_second, *fetched = call(
         first_kernel,
         [
             density.reshape(cells, width),
@@ -393,7 +395,12 @@
         [(own, "gx", pltpu.VMEM), (sends, "gx", pltpu.VMEM)],
         [(5 * cells, width), (cells, width), (2, 5 * cells), (2, 5 * cells)],
         [pltpu.VMEM((5 * cells, width), jnp.float32)],
-        ahead=[(within, "gy"), (last, "gy")],
+        ahead=[
+            (applied, "gx", pltpu.VMEM),
+            (ends, "gy", pltpu.SMEM),
+            (within, "gy", pltpu.SMEM),
+            (last, "gy", pltpu.SMEM),
+        ],
         inside=False,
     )
     second = lax.ppermute(to_second, "gx", pairs(1, columns))
@@ -401,13 +408,14 @@
     advanced, summed, first_rows, second_rows = call(
         second_kernel,
         [partial, fluid, first, second],
-        [(applied, "gx", pltpu.VMEM), (ends, "gy", pltpu.SMEM)],
+        [],
         [
             (5 * cells, width),
             (2 * lines, width),
             (reach * lines, width),
             (reach * lines, width),
         ],
+        rows=[(fetched[0], pltpu.VMEM), (fetched[1], pltpu.SMEM)],
     )
     first_rows = lax.ppermute(first_rows, "gy", pairs(0, parts))
     second_rows = lax.ppermute(second_rows, "gy", pairs(1, parts))
@@ -415,7 +423,11 @@
     far = [[g * inner + k for g in range(outer)] for k in range(inner)]
     gathered = lax.all_gather(summed, "gy", axis_index_groups=near)
     prefix, slab = call(
-        third_kernel, [gathered], [], [(2 * lines, width), (outer, lines, width)], rows=[within_row]
+        third_kernel,
+        [gathered],
+        [],
+        [(2 * lines, width), (outer, lines, width)],
+        rows=[(fetched[2], pltpu.SMEM)],
     )
     exchanged = lax.all_to_all(slab, "gy", 0, 0, axis_index_groups=far)
     (result,) = call(
@@ -423,7 +435,7 @@
         [advanced, fluid, first_rows, second_rows, prefix, exchanged],
         [],
         [(5 * cells, width)],
-        rows=[last_row],
+        rows=[(fetched[3], pltpu.SMEM)],
         kept=False,
     )
     return result.reshape(5, planes, transverse, width)

time: 67 us -> 66.2 us (0.988)
  Pallas kernels: 5.41 us -> 4.66 us
    pallas_call x4, Pallas kernels: 5.41 us -> 4.66 us  [call(): pl.pallas_call(run, in_specs=[vmem] * len(arrays) + [pl.BlockSpec(memory_...]
where the time goes in v5:
time: 66.2 us; the launch traced here: 65.8 us
  blocking collectives  35.3 us (53%)
  starting transfers between devices  16.6 us (25%)
  waiting for transfers between devices  9.24 us (14%)
  Pallas kernels  4.66 us (7%)
    all_gather x1, blocking collectives, body(): gathered = lax.all_gather(summed, 'gy', axis_index_groups=near)  35.3 us
    all_to_all x1, starting transfers between devices, body(): exchanged = lax.all_to_all(slab, 'gy', 0, 0, axis_index_groups=far)  7.21 us
    ppermute x1, waiting for transfers between devices, body(): second_rows = lax.ppermute(second_rows, 'gy', pairs(1, parts))  5.25 us
    pallas_call x4, Pallas kernels, call(): pl.pallas_call(run, in_specs=[vmem] * len(arrays) + [pl.BlockSpec(memory_...  4.66 us
    ppermute x1, starting transfers between devices, body(): second = lax.ppermute(to_second, 'gx', pairs(1, columns))  2.84 us
    ppermute x1, starting transfers between devices, body(): second_rows = lax.ppermute(second_rows, 'gy', pairs(1, parts))  2.71 us
    ppermute x1, waiting for transfers between devices, body(): second = lax.ppermute(to_second, 'gx', pairs(1, columns))  2.08 us
    ppermute x1, starting transfers between devices, body(): first = lax.ppermute(to_first, 'gx', pairs(0, columns))  1.92 us
  transfers between devices with their start and end apart: 5, of which 3 were waited for; matrix products, arithmetic and copies ran while one was open for 0% of the time, Pallas kernels for 0%

profile of v5, /device:TPU:38, one launch (start us, length us, event | category | flops | bytes accessed | tf_op | source)
XLA Modules:
  0.0 65.8 jit_solution(8745633664240589847)
XLA Ops:
  0.0 2.3 %shard_map.100 = (f32[640,128]{1,0:T(8,128)S(1)}, f32[128,128]{1,0:T(8,128)S(1)}, f32[2,640]{1,0:T(2,128)S(1)}, f32[2,640]{1,0:T(2,128)S(1)}, bf16[16,128]{1,0:T...) custom-call(f32[128,128]{1,0:T(8,128)} %bitcast.8, f32[384,128]{1,0:T(8,128)} %bitcast.7, ...), custom_call_target="tpu_custom_call" | custom-call | tf_op jit(solution)/shard_map/pallas_call | solution.py:352
  2.3 1.9 %collective-permute-start = (f32[2,640]{1,0:T(2,128)S(1)}, f32[2,640]{1,0:T(2,128)S(1)}, u32[]{:S(2)}, u32[]{:S(2)}) collective-permute-start(f32[2,640]{1,0:T(2,128)S(1)} %get-tuple-element.21), channel_id=1, source_target_pairs={{0,96},{96,0},{192,288},{288,192},{384,480},{480,384},{576,672},{6... | collective-permute-start | bytes 15368 | tf_op jit(solution)/shard_map/ppermute | solution.py:407
  4.2 2.8 %collective-permute-start.1 = (f32[2,640]{1,0:T(2,128)S(1)}, f32[2,640]{1,0:T(2,128)S(1)}, u32[]{:S(2)}, u32[]{:S(2)}) collective-permute-start(f32[2,640]{1,0:T(2,128)S(1)} %get-tuple-element.22), channel_id=1, source_target_pairs={{96,192},{192,96},{288,384},{384,288},{480,576},{576,480},{97,193}... | collective-permute-start | bytes 15368 | tf_op jit(solution)/shard_map/ppermute | solution.py:406
  7.1 0.0 collective-permute-done.refs_2_
  7.1 2.1 %collective-permute-done.1.refs_3_ = f32[2,640]{1,0:T(2,128)S(1)} collective-permute-done((f32[2,640]{1,0:T(2,128)S(1)}, f32[2,640]{1,0:T(2,128)S(1)}, u32[]{:S(2)}, u32[]{:S(2)}) %collective-permute-start.1) | collective-permute-done | bytes 5152 | tf_op jit(solution)/shard_map/ppermute | solution.py:406
  9.2 0.3 shard_map.101
  9.5 35.3 %all-gather = f32[960,128]{1,0:T(8,128)S(1)} all-gather(f32[80,128]{1,0:T(8,128)S(1)} %get-tuple-element.28), channel_id=2, replica_groups={{0,1,2,3,4,5,6,7,8,9,10,11},{12,13,14,15,16,17,18,19,20,21,22,23},{24,2..., dimensions={0}, use_global_device_ids=true | all-gather | bytes 532480 | tf_op jit(solution)/shard_map/all_gather | solution.py:424
  44.8 0.7 %shard_map.102 = (f32[80,128]{1,0:T(8,128)S(1)}, f32[8,40,128]{2,1,0:T(8,128)}) custom-call(f32[12,80,128]{2,1,0:T(8,128)S(1)} %bitcast.6, f32[1,128]{1,0:T(1,128)S(4)} %get-tuple-element.29.refs_1_), custom_call_target="tpu_custom_call" | custom-call | tf_op jit(solution)/shard_map/pallas_call | solution.py:352
  45.5 7.2 %all-to-all-start = ((f32[8,40,128]{2,1,0:T(8,128)}), f32[8,40,128]{2,1,0:T(8,128)S(1)}, u32[]{:S(2)}, u32[]{:S(2)}) async-start(f32[8,40,128]{2,1,0:T(8,128)} %get-tuple-element.31), calls=%async_computation | async-start | bytes 327680 | tf_op jit(solution)/shard_map/all_to_all | solution.py:432
  52.7 1.9 %collective-permute-start.2 = (f32[200,128]{1,0:T(8,128)S(1)}, f32[200,128]{1,0:T(8,128)S(1)}, u32[]{:S(2)}, u32[]{:S(2)}) collective-permute-start(f32[200,128]{1,0:T(8,128)S(1)} %get-tuple-element.26), channel_id=1, source_target_pairs={{0,1},{1,0},{2,3},{3,2},{4,5},{5,4},{6,7},{7,6},{8,9},{9,8},{10,11... | collective-permute-start | bytes 307208 | tf_op jit(solution)/shard_map/ppermute | solution.py:420
  54.6 2.7 %collective-permute-start.3 = (f32[200,128]{1,0:T(8,128)S(1)}, f32[200,128]{1,0:T(8,128)S(1)}, u32[]{:S(2)}, u32[]{:S(2)}) collective-permute-start(f32[200,128]{1,0:T(8,128)S(1)} %get-tuple-element.27), channel_id=1, source_target_pairs={{1,2},{2,1},{3,4},{4,3},{5,6},{6,5},{7,8},{8,7},{9,10},{10,9},{11,... | collective-permute-start | bytes 307208 | tf_op jit(solution)/shard_map/ppermute | solution.py:421
  57.3 1.9 %collective-permute-done.2.refs_2_ = f32[200,128]{1,0:T(8,128)S(1)} collective-permute-done((f32[200,128]{1,0:T(8,128)S(1)}, f32[200,128]{1,0:T(8,128)S(1)}, u32[]{:S(2)}, u32[]{:S(2)}) %collective-permute-start.2) | collective-permute-done | bytes 102432 | tf_op jit(solution)/shard_map/ppermute | solution.py:420
  59.2 5.2 %collective-permute-done.3.refs_3_ = f32[200,128]{1,0:T(8,128)S(1)} collective-permute-done((f32[200,128]{1,0:T(8,128)S(1)}, f32[200,128]{1,0:T(8,128)S(1)}, u32[]{:S(2)}, u32[]{:S(2)}) %collective-permute-start.3) | collective-permute-done | bytes 102432 | tf_op jit(solution)/shard_map/ppermute | solution.py:421
  64.5 0.0 all-to-all-done.refs_5_
  64.5 1.4 %shard_map.103 = f32[640,128]{1,0:T(8,128)} custom-call(f32[640,128]{1,0:T(8,128)S(1)} %get-tuple-element.25.refs_0_, f32[128,128]{1,0:T(8,128)S(1)} %get-tuple-element.20.refs_1_, f32[200,128]{1,0:T(8,128)S(1)} %collective-permute-done.2.refs_2_, f32[200,128]{1,0:T(8,128)S(1)} %collective-permute-done.3.refs_3_, f32[80,128]{1,0:T(8,128)S(1)} %get-tuple-element.30.refs_4_, ...), custom_call_target="tpu_custom_call" | custom-call | tf_op jit(solution)/shard_map/pallas_call | solution.py:352
Async XLA Ops:
  2.3 4.8 %collective-permute-start = (f32[2,640]{1,0:T(2,128)S(1)}, f32[2,640]{1,0:T(2,128)S(1)}, u32[]{:S(2)}, u32[]{:S(2)}) collective-permute-start(f32[2,640]{1,0:T(2,128)S(1)} %get-tuple-element.21), channel_id=1, source_target_pairs={{0,96},{96,0},{192,288},{288,192},{384,480},{480,384},{576,672},{6... | collective-permute-start | bytes 15368 | tf_op jit(solution)/shard_map/ppermute | solution.py:407
  4.2 4.9 %collective-permute-start.1 = (f32[2,640]{1,0:T(2,128)S(1)}, f32[2,640]{1,0:T(2,128)S(1)}, u32[]{:S(2)}, u32[]{:S(2)}) collective-permute-start(f32[2,640]{1,0:T(2,128)S(1)} %get-tuple-element.22), channel_id=1, source_target_pairs={{96,192},{192,96},{288,384},{384,288},{480,576},{576,480},{97,193}... | collective-permute-start | bytes 15368 | tf_op jit(solution)/shard_map/ppermute | solution.py:406
  45.5 19.0 %all-to-all-start = ((f32[8,40,128]{2,1,0:T(8,128)}), f32[8,40,128]{2,1,0:T(8,128)S(1)}, u32[]{:S(2)}, u32[]{:S(2)}) async-start(f32[8,40,128]{2,1,0:T(8,128)} %get-tuple-element.31), calls=%async_computation | async-start | bytes 327680 | tf_op jit(solution)/shard_map/all_to_all | solution.py:432
  52.7 6.5 %collective-permute-start.2 = (f32[200,128]{1,0:T(8,128)S(1)}, f32[200,128]{1,0:T(8,128)S(1)}, u32[]{:S(2)}, u32[]{:S(2)}) collective-permute-start(f32[200,128]{1,0:T(8,128)S(1)} %get-tuple-element.26), channel_id=1, source_target_pairs={{0,1},{1,0},{2,3},{3,2},{4,5},{5,4},{6,7},{7,6},{8,9},{9,8},{10,11... | collective-permute-start | bytes 307208 | tf_op jit(solution)/shard_map/ppermute | solution.py:420
  54.6 9.9 %collective-permute-start.3 = (f32[200,128]{1,0:T(8,128)S(1)}, f32[200,128]{1,0:T(8,128)S(1)}, u32[]{:S(2)}, u32[]{:S(2)}) collective-permute-start(f32[200,128]{1,0:T(8,128)S(1)} %get-tuple-element.27), channel_id=1, source_target_pairs={{1,2},{2,1},{3,4},{4,3},{5,6},{6,5},{7,8},{8,7},{9,10},{10,9},{11,... | collective-permute-start | bytes 307208 | tf_op jit(solution)/shard_map/ppermute | solution.py:421
